TPU v7x, 512 devices: a whole 4x4x16 slice. The times are simulated.
512 devices in a mesh: dp: 64 (over x, z), inner: 8 (over y, core).
Axes of the slice: x: 4, y: 4, z: 16, core: 2. Of those that a mesh axis runs over, the one named last changes fastest.
Arguments:
- tokens: bfloat16 [4096, 2880], P(('dp', 'inner')), may hold values from -6 to 6
- segments: int32 [4096], P(('dp', 'inner')), may hold values from 0 to 63, never falling along the last dimension, each value on 1 to 256 neighbouring positions
- attn_gain: float32 [2880], replicated, may hold values from 0.5 to 1.5
- w_query: bfloat16 [2880, 4096], P('dp', 'inner'), may hold values from -0.109375 to 0.109375
- w_keyval: bfloat16 [2880, 1024], P('dp', 'inner'), may hold values from -0.109375 to 0.109375
- sink_logits: float32 [64], P('inner'), may hold values from -1 to 3
- w_out: bfloat16 [4096, 2880], P('inner', 'dp'), may hold values from -0.09375 to 0.09375
- moe_gain: float32 [2880], replicated, may hold values from 0.5 to 1.5
- w_router: bfloat16 [2880, 32], replicated, may hold values from -0.109375 to 0.109375
- routes: int32 [4096, 4], P(('dp', 'inner')), may hold values from 0 to 31, all different within a row; in each aligned block of 8 rows (0 to 7, 8 to 15, ...) at most 2 rows name the same one
- w_gate_up: bfloat16 [92160, 5760], P('dp', 'inner'), may hold values from -0.109375 to 0.109375
- b_gate_up: float32 [32, 5760], P(None, 'inner'), may hold values from -3 to 3
- w_down: bfloat16 [2880, 92160], P('inner', 'dp'), may hold values from -0.109375 to 0.109375
- b_down: float32 [32, 2880], replicated, may hold values from -3 to 3
Outputs:
- layer_out: bfloat16 [4096, 2880], P(('dp', 'inner'))
Inputs may be any that keep to these rules, and one draw needn't show every extreme that they name: `routes`: in each aligned block of 8 rows (the rows of one device) no expert is named by more than 2 rows, a bound that some block reaches; the 4 experts of a row differ. `segments`: never falling along the tokens; each segment holds 1 to 256 tokens, one exactly 256.
All inputs are finite; a program needn't handle non-finite values.
Results may differ from a plain program's by a relative error of at most 0.018.
Values may be sent and summed in bfloat16 or wider, within the bound.
A program may use at most 64 MiB of HBM per device.

v0:
```python
import jax
import jax.numpy as jnp
from jax import lax
from jax.sharding import PartitionSpec as P

HEAD_DIM = 64
WINDOW = 128


EPSILON = 1e-05
ROPE_BASE = 150000.0
CLAMP_LIMIT = 7.0
GLU_SLOPE = 1.702


def passed_along(value, axis, steps):
    count = lax.axis_size(axis)
    initial, last = (max(0, -steps), min(count, count - steps))
    return lax.ppermute(value, axis, [(source, source + steps) for source in range(initial, last)])


def from_partner(value, axis, apart):
    mask = 2**apart
    pairs = [(source, source ^ mask) for source in range(lax.axis_size(axis))]
    return lax.ppermute(value, axis, pairs)


def rms_scale(row_block, gain_vector):
    values = row_block.astype(jnp.float32)
    mean_square = jnp.mean(values * values, axis=-1, keepdims=True)
    return (values * lax.rsqrt(mean_square + EPSILON) * gain_vector).astype(jnp.bfloat16)


def rotate(values, positions):
    half_dim = values.shape[-1] // 2
    frequency = ROPE_BASE ** (-2.0 * jnp.arange(half_dim, dtype=jnp.float32) / values.shape[-1])
    angles = positions.astype(jnp.float32)[:, None] * frequency[None, :]
    cosine = jnp.cos(angles)[:, None, :]
    sine_part = jnp.sin(angles)[:, None, :]
    first_half = values[..., :half_dim]
    second = values[..., half_dim:]
    return jnp.concatenate(
        [first_half * cosine - second * sine_part, second * cosine + first_half * sine_part],
        axis=-1,
    )


def attend(queries, key_block, value_block, sink_heads, query_pos, key_pos, query_seg, key_seg):
    scores = jnp.einsum(
        "qgph,kgh->gpqk", queries, key_block, preferred_element_type=jnp.float32
    ) * HEAD_DIM ** (-0.5)
    distance = query_pos[:, None] - key_pos[None, :]
    allowed = (
        (distance >= 0)
        & (distance < WINDOW)
        & (key_pos[None, :] >= 0)
        & (query_seg[:, None] == key_seg[None, :])
    )
    scores = jnp.where(allowed[None, None], scores, -jnp.inf)
    row_max = jnp.maximum(jnp.max(scores, axis=-1), sink_heads[:, :, None])
    weights = jnp.exp(scores - row_max[..., None])
    denominator = jnp.sum(weights, axis=-1) + jnp.exp(sink_heads[:, :, None] - row_max)
    probabilities = (weights / denominator[..., None]).astype(jnp.bfloat16)
    mixed_heads = jnp.einsum(
        "gpqk,kgh->qgph", probabilities, value_block, preferred_element_type=jnp.float32
    )
    return mixed_heads.astype(jnp.bfloat16)


def slot_numbers(route_block, expert_count):
    flat_routes = route_block.reshape(-1)
    onehot = (flat_routes[:, None] == jnp.arange(expert_count, dtype=jnp.int32)[None, :]).astype(
        jnp.int32
    )
    earlier = jnp.cumsum(onehot, axis=0) - onehot
    return jnp.sum(earlier * onehot, axis=1).reshape(route_block.shape)


def route_mix(moe_rows, w_router, route_block):
    expert_count = w_router.shape[1]
    logits = jnp.dot(moe_rows, w_router, preferred_element_type=jnp.float32)
    matches = route_block[:, :, None] == jnp.arange(expert_count, dtype=jnp.int32)[None, None, :]
    chosen = jnp.sum(jnp.where(matches, logits[:, None, :], 0.0), axis=-1)
    return (jax.nn.softmax(chosen, axis=-1), matches)


def send_table(targets, length):
    columns = jnp.arange(length, dtype=jnp.int32)
    return jnp.any(columns[:, None, None] == targets[None, :, :], axis=-1).astype(jnp.bfloat16)


def spread_rows(table, row_block, dp_count):
    placed = jnp.dot(table, row_block, preferred_element_type=jnp.float32)
    return placed.astype(jnp.bfloat16).reshape(dp_count, -1, row_block.shape[1])


def join_rows(returned):
    dp_count, span, width = returned.shape
    return returned.reshape(-1, width)


def pick_rows(returned, targets, weights):
    taken = jnp.take(returned, targets, axis=0).astype(jnp.float32)
    return jnp.sum(weights[:, :, None] * taken, axis=1)


def activate(gate_up):
    gate_part = jnp.minimum(gate_up[:, 0::2], CLAMP_LIMIT)
    up_part = jnp.clip(gate_up[:, 1::2], -CLAMP_LIMIT, CLAMP_LIMIT)
    return ((up_part + 1.0) * gate_part * jax.nn.sigmoid(GLU_SLOPE * gate_part)).astype(
        jnp.bfloat16
    )


def per_device(
    tokens,
    segments,
    attn_gain,
    w_query,
    w_keyval,
    sink_logits,
    w_out,
    moe_gain,
    w_router,
    routes,
    w_gate_up,
    b_gate_up,
    w_down,
    b_down,
):
    tok_rows, model_width = tokens.shape
    inner_count = lax.axis_size("inner")
    dp_count = lax.axis_size("dp")
    dp_index = lax.axis_index("dp")
    inner_index = lax.axis_index("inner")
    group_rows = tok_rows * inner_count
    local_heads = w_query.shape[1] // HEAD_DIM
    local_kv = w_keyval.shape[1] // (2 * HEAD_DIM)
    per_kv = local_heads // local_kv
    group_start = dp_index * group_rows
    attn_in = rms_scale(tokens, attn_gain)
    group_in, group_segments = (
        lax.all_gather(attn_in, "inner", axis=0, tiled=True),
        lax.all_gather(segments, "inner", axis=0, tiled=True),
    )
    query_acc = jnp.dot(
        group_in,
        lax.all_gather(w_query, "dp", axis=0, tiled=True),
        preferred_element_type=jnp.float32,
    )
    keyval_acc = jnp.dot(
        group_in,
        lax.all_gather(w_keyval, "dp", axis=0, tiled=True),
        preferred_element_type=jnp.float32,
    )
    positions = group_start + jnp.arange(group_rows, dtype=jnp.int32)
    queries = rotate(query_acc.reshape(group_rows, local_heads, HEAD_DIM), positions).astype(
        jnp.bfloat16
    )
    queries = queries.reshape(group_rows, local_kv, per_kv, HEAD_DIM)
    keyval = keyval_acc.reshape(group_rows, local_kv, 2, HEAD_DIM)
    key_rows = rotate(keyval[:, :, 0], positions).astype(jnp.bfloat16)
    value_rows = keyval[:, :, 1].astype(jnp.bfloat16)
    packed = jnp.concatenate(
        [key_rows.reshape(group_rows, -1), value_rows.reshape(group_rows, -1)], axis=1
    )
    reach = (WINDOW + group_rows - 2) // group_rows
    packed_parts = []
    segment_parts = []
    for stride in range(reach, 0, -1):
        moved_keys, moved_segments = passed_along((packed, group_segments), "dp", stride)
        packed_parts.append(moved_keys)
        segment_parts.append(moved_segments)
    window_keys = jnp.concatenate(packed_parts + [packed], axis=0)
    window_segments = jnp.concatenate(segment_parts + [group_segments], axis=0)
    key_count = window_keys.shape[0]
    key_pos = group_start - reach * group_rows + jnp.arange(key_count, dtype=jnp.int32)
    half_cols = local_kv * HEAD_DIM
    key_block = window_keys[:, :half_cols].reshape(key_count, local_kv, HEAD_DIM)
    value_block = window_keys[:, half_cols:].reshape(key_count, local_kv, HEAD_DIM)
    attended = attend(
        queries,
        key_block,
        value_block,
        sink_logits.reshape(local_kv, per_kv),
        positions,
        key_pos,
        group_segments,
        window_segments,
    )
    attended = attended.reshape(group_rows, local_heads * HEAD_DIM)
    out_full = lax.all_gather(w_out, "dp", axis=1, tiled=True)
    row_block = attended
    attn_sum = lax.psum_scatter(
        jnp.dot(row_block, out_full, preferred_element_type=jnp.float32).astype(jnp.bfloat16),
        "inner",
        scatter_dimension=0,
        tiled=True,
    ).astype(jnp.float32)
    residual = (tokens.astype(jnp.float32) + attn_sum).astype(jnp.bfloat16)
    moe_in = rms_scale(residual, moe_gain)
    expert_count = w_router.shape[1]
    capacity = 16 * tok_rows // dp_count
    half_cap = capacity // 2
    parity = dp_index % 2
    expert_id = dp_index // 2
    half_rows = w_gate_up.shape[0]
    bias_row = lax.dynamic_slice_in_dim(b_gate_up, expert_id, 1, 0)
    gate_other, down_other = from_partner((w_gate_up, w_down), "dp", 0)
    mix, matches = route_mix(moe_in, w_router, routes)
    expert_mix = jnp.sum(jnp.where(matches, mix[:, :, None], 0.0), axis=1)
    bias_term = jnp.dot(expert_mix, b_down, precision=lax.Precision.HIGHEST)
    slot_index = slot_numbers(routes, expert_count)
    source_flip = (dp_index + inner_index) % 2
    slot_half = (slot_index // half_cap + source_flip) % 2
    targets = routes * capacity + slot_half * half_cap + slot_index % half_cap
    length = expert_count * capacity
    outgoing = spread_rows(send_table(targets, length), moe_in, dp_count)
    received = lax.all_to_all(outgoing, "dp", split_axis=0, concat_axis=0, tiled=True)
    expert_rows = lax.all_gather(received, "inner", axis=0, tiled=True)
    row_block = expert_rows.reshape(-1, expert_rows.shape[-1])
    own_cols = lax.dynamic_slice_in_dim(row_block, parity * half_rows, half_rows, 1)
    other_cols = lax.dynamic_slice_in_dim(row_block, (1 - parity) * half_rows, half_rows, 1)
    own_part = jnp.dot(own_cols, w_gate_up, preferred_element_type=jnp.float32).astype(jnp.bfloat16)
    other_part = jnp.dot(other_cols, gate_other, preferred_element_type=jnp.float32).astype(
        jnp.bfloat16
    )
    own_part, other_part = lax.optimization_barrier((own_part, other_part))
    hidden = activate(own_part.astype(jnp.float32) + other_part.astype(jnp.float32) + bias_row)
    own_out = jnp.dot(hidden, w_down, preferred_element_type=jnp.float32)
    other_out = jnp.dot(hidden, down_other, preferred_element_type=jnp.float32)
    joined = jnp.where(
        parity == 0,
        jnp.concatenate([own_out, other_out], axis=1),
        jnp.concatenate([other_out, own_out], axis=1),
    )
    partial_value = joined.astype(jnp.bfloat16)
    summed = lax.psum_scatter(partial_value, "inner", scatter_dimension=0, tiled=True).astype(
        jnp.float32
    )
    returned = lax.all_to_all(
        summed.reshape(dp_count, -1, summed.shape[-1]).astype(jnp.bfloat16),
        "dp",
        split_axis=0,
        concat_axis=0,
        tiled=True,
    ).astype(jnp.float32)
    moe_sum = pick_rows(join_rows(returned), targets, mix)
    return (residual.astype(jnp.float32) + moe_sum + bias_term).astype(jnp.bfloat16)


def solution(mesh):
    return jax.shard_map(
        per_device,
        mesh=mesh,
        in_specs=(
            P(("dp", "inner"), None),
            P(("dp", "inner")),
            P(),
            P("dp", "inner"),
            P("dp", "inner"),
            P("inner"),
            P("inner", "dp"),
            P(),
            P(),
            P(("dp", "inner"), None),
            P("dp", "inner"),
            P(None, "inner"),
            P("inner", "dp"),
            P(),
        ),
        out_specs=P(("dp", "inner"), None),
        check_vma=False,
    )
```

profile of v0, /device:TPU:1, one launch (start us, length us, event | category | flops | bytes accessed | tf_op | source)
XLA Modules:
  0.0 584.8 jit_solution(14651983438943799095)
XLA Ops:
  8.1 84.7 %all-gather = bf16[64,45,128]{2,1,0:T(8,128)(2,1)S(1)} all-gather(bf16[1,45,128]{2,1,0:T(8,128)(2,1)} %bitcast.79), channel_id=1, replica_groups=mesh['dp'=64,'inner'=8] {'dp'}, dimensions={0}, use_global_device_ids=true | all-gather | bytes 748800 | tf_op jit(solution)/shard_map/all_gather | solution.py:153
  93.3 37.2 %all_gather.18 = bf16[64,2880]{1,0:T(8,128)(2,1)S(1)} all-gather(bf16[8,2880]{1,0:T(8,128)(2,1)S(1)} %fusion.24), channel_id=1, replica_groups=mesh['dp'=64,'inner'=8] {'inner'}, dimensions={0}, use_global_device_ids=true | all-gather | bytes 414720 | tf_op jit(solution)/shard_map/all_gather | solution.py:143
  131.9 1.9 collective-permute-start
  133.9 2.7 collective-permute-start.1
  138.1 7.9 %all-reduce = s32[64]{0:T(128)S(1)} all-reduce(s32[64]{0:T(128)S(1)} %dynamic-update-slice), channel_id=1, replica_groups=mesh['dp'=64,'inner'=8] {'inner'}, use_global_device_ids=true, to_apply=%add | all-reduce | flops 64 | bytes 512
  146.0 3.8 collective-permute-start.2
  149.8 4.0 collective-permute-start.3
  157.3 3.0 reshape.408
  160.3 1.6 fusion.62
  164.3 128.8 %all-gather.11.cloned.1.call-done = bf16[64,45,512]{2,1,0:T(8,128)(2,1)} async-done(((bf16[1,45,512]{2,1,0:T(8,128)(2,1)}), bf16[64,45,512]{2,1,0:T(8,128)(2,1)}) %all-gather.11.cloned.1.call-update) | async-done | bytes 2949136 | tf_op jit(solution)/shard_map/all_gather | solution.py:192
  293.1 3.0 reshape.410
  296.2 1.8 convolution_convert_fusion.1
  298.9 76.1 %all-reduce.4.cloned.1.call-done = bf16[64,2880]{1,0:T(8,128)(2,1)} async-done(((bf16[64,2880]{1,0:T(8,128)(2,1)}), bf16[64,2880]{1,0:T(8,128)(2,1)}) %all-reduce.4.cloned.1.call-update) | async-done | bytes 368656
  375.1 0.9 fusion.26
  378.2 35.9 %all_to_all.10 = bf16[64,2,1440]{2,1,0:T(2,128)(2,1)S(1)} all-to-all(bf16[64,2,1440]{2,1,0:T(2,128)(2,1)S(1)} %reshape.419), channel_id=1, replica_groups=mesh['dp'=64,'inner'=8] {'dp'}, dimensions={0} | all-to-all | bytes 737280 | tf_op jit(solution)/shard_map/all_to_all | solution.py:219
  415.5 4.1 collective-permute-start.4
  419.6 2.1 collective-permute-start.5
  422.5 26.1 %all-gather.7.cloned.1.call-done = bf16[512,1,2880]{2,0,1:T(8,128)(2,1)} async-done(((bf16[64,1,2880]{2,0,1:T(8,128)(2,1)}), bf16[512,1,2880]{2,0,1:T(8,128)(2,1)}) %all-gather.7.cloned.1.call-update) | async-done | bytes 2949136 | tf_op jit(solution)/shard_map/all_gather | solution.py:220
  448.6 3.9 fusion.9
  452.5 10.7 %collective-permute-done.4 = bf16[1440,720]{1,0:T(8,128)(2,1)S(1)} collective-permute-done((bf16[1440,720]{1,0:T(8,128)(2,1)}, bf16[1440,720]{1,0:T(8,128)(2,1)S(1)}, u32[]{:S(2)}, u32[]{:S(2)}) %collective-permute-start.4) | collective-permute-done | bytes 2073632 | tf_op jit(solution)/shard_map/ppermute | solution.py:25
  463.2 1.6 fusion.12
  466.8 2.2 fusion.63
  469.1 17.9 %collective-permute-done.5 = bf16[360,1440]{1,0:T(8,128)(2,1)} collective-permute-done((bf16[360,1440]{1,0:T(8,128)(2,1)}, bf16[360,1440]{1,0:T(8,128)(2,1)}, u32[]{:S(2)}, u32[]{:S(2)}) %collective-permute-start.5) | collective-permute-done | bytes 1036832 | tf_op jit(solution)/shard_map/ppermute | solution.py:25
  486.9 2.2 fusion.64
  489.2 0.9 fusion
  490.1 3.0 copy.79
  493.1 42.8 %reduce-scatter.4.cloned.1.call-done = bf16[64,2880]{1,0:T(8,128)(2,1)} async-done(((bf16[512,2880]{1,0:T(8,128)(2,1)}), bf16[64,2880]{1,0:T(8,128)(2,1)}) %reduce-scatter.4.cloned.1.call-update) | async-done | bytes 368656
  535.9 1.4 copy.80
  537.3 1.4 reduce.5
  538.9 1.2 reshape.421
  540.2 14.4 %all-to-all-start.1 = ((bf16[64,2,1440]{2,1,0:T(2,128)(2,1)}), bf16[64,2,1440]{2,1,0:T(2,128)(2,1)S(1)}, u32[]{:S(2)}, u32[]{:S(2)}) async-start(bf16[64,2,1440]{2,1,0:T(2,128)(2,1)} %reshape.421), calls=%async_computation.1 | async-start | bytes 786432 | tf_op jit(solution)/shard_map/all_to_all | solution.py:241
  555.3 20.3 %all-to-all-done.1 = bf16[64,2,1440]{2,1,0:T(2,128)(2,1)S(1)} async-done(((bf16[64,2,1440]{2,1,0:T(2,128)(2,1)}), bf16[64,2,1440]{2,1,0:T(2,128)(2,1)S(1)}, u32[]{:S(2)}, u32[]{:S(2)}) %all-to-all-start.1) | async-done | bytes 368672 | tf_op jit(solution)/shard_map/all_to_all | solution.py:241
  (115 shorter events, 20.0 us)
Async XLA Ops:
  6.5 570.8 %copy-start = (f32[32,2880]{1,0:T(8,128)S(1)}, f32[32,2880]{1,0:T(8,128)}, u32[]{:S(2)}) copy-start(f32[32,2880]{1,0:T(8,128)} %param.27) | copy-start | bytes 1105924
  6.5 86.5 %copy-start.2 = (bf16[8,2880]{1,0:T(8,128)(2,1)S(1)}, bf16[8,2880]{1,0:T(8,128)(2,1)}, u32[]{:S(2)}) copy-start(bf16[8,2880]{1,0:T(8,128)(2,1)} %param.14) | copy-start | bytes 138244
  6.5 86.7 %copy-start.10 = (f32[2880]{0:T(1024)S(1)}, f32[2880]{0:T(1024)}, u32[]{:S(2)}) copy-start(f32[2880]{0:T(1024)} %param.16) | copy-start | bytes 34564
  6.5 150.7 %all-gather.9.cloned.1.call-start = ((), (), s32[]{:S(2)}) async-start(), calls=%async_computation.4 | async-start | bytes 3194880 | tf_op jit(solution)/shard_map/all_gather | solution.py:148
  7.3 129.3 %copy-start.12 = (u32[512]{0:T(512)S(1)}, u32[512]{0:T(512)}, u32[]{:S(2)}) copy-start(u32[512]{0:T(512)} %constant.142) | copy-start | bytes 6148
  7.3 130.6 %copy-start.15 = (s32[8]{0:T(128)S(1)}, s32[8]{0:T(128)}, u32[]{:S(2)}) copy-start(s32[8]{0:T(128)} %param.15) | copy-start | bytes 100
  7.3 285.8 %all-gather.11.cloned.1.call-start = ((), (), s32[]{:S(2)}) async-start(), calls=%async_computation.5 | async-start | bytes 3194880 | tf_op jit(solution)/shard_map/all_gather | solution.py:192
  7.3 146.5 %copy-start.6 = (s32[8,4]{0,1:T(4,128)S(1)}, s32[8,4]{0,1:T(4,128)}, u32[]{:S(2)}) copy-start(s32[8,4]{0,1:T(4,128)} %param.23) | copy-start | bytes 388
  8.0 367.0 %all-reduce.4.cloned.1.call-start = ((), (), s32[]{:S(2)}) async-start(), calls=%async_computation.7 | async-start | bytes 753664
  130.5 0.8 copy-start.1
  131.9 24.6 %collective-permute-start = (bf16[64,128]{0,1:T(8,128)(2,1)S(1)}, bf16[64,128]{0,1:T(8,128)(2,1)S(1)}, u32[]{:S(2)}, u32[]{:S(2)}) collective-permute-start(bf16[64,128]{0,1:T(8,128)(2,1)S(1)} %pad_maximum_fusion), channel_id=1, source_target_pairs={{0,16},{8,24},{16,32},{24,40},{32,48},{40,56},{48,64},{56,72},{64,... | collective-permute-start | bytes 49160 | tf_op jit(solution)/shard_map/ppermute | solution.py:19
  133.9 22.7 %collective-permute-start.1 = (bf16[64,128]{0,1:T(8,128)(2,1)S(1)}, bf16[64,128]{0,1:T(8,128)(2,1)S(1)}, u32[]{:S(2)}, u32[]{:S(2)}) collective-permute-start(bf16[64,128]{0,1:T(8,128)(2,1)S(1)} %pad_maximum_fusion), channel_id=1, source_target_pairs={{0,8},{8,16},{16,24},{24,32},{32,40},{40,48},{48,56},{56,64},{64,7... | collective-permute-start | bytes 49160 | tf_op jit(solution)/shard_map/ppermute | solution.py:19
  146.0 10.4 %collective-permute-start.2 = (s32[64]{0:T(128)S(1)}, s32[64]{0:T(128)S(1)}, u32[]{:S(2)}, u32[]{:S(2)}) collective-permute-start(s32[64]{0:T(128)S(1)} %all-reduce), channel_id=1, source_target_pairs={{0,16},{8,24},{16,32},{24,40},{32,48},{40,56},{48,64},{56,72},{64,... | collective-permute-start | bytes 776 | tf_op jit(solution)/shard_map/ppermute | solution.py:19
  149.8 6.6 %collective-permute-start.3 = (s32[64]{0:T(128)S(1)}, s32[64]{0:T(128)S(1)}, u32[]{:S(2)}, u32[]{:S(2)}) collective-permute-start(s32[64]{0:T(128)S(1)} %all-reduce), channel_id=1, source_target_pairs={{0,8},{8,16},{16,24},{24,32},{32,40},{40,48},{48,56},{56,64},{64,7... | collective-permute-start | bytes 776 | tf_op jit(solution)/shard_map/ppermute | solution.py:19
  153.9 0.6 copy-start.4
  162.0 1.1 copy-start.3
  162.0 1.5 copy-start.11
  296.2 1.9 copy-start.5
  296.2 1.9 copy-start.8
  296.2 79.8 %copy-start.9 = (f32[2880]{0:T(1024)S(1)}, f32[2880]{0:T(1024)}, u32[]{:S(2)}) copy-start(f32[2880]{0:T(1024)} %param.21) | copy-start | bytes 34564
  298.0 150.6 %all-gather.7.cloned.1.call-start = ((), (), s32[]{:S(2)}) async-start(), calls=%async_computation.3 | async-start | bytes 3391488 | tf_op jit(solution)/shard_map/all_gather | solution.py:220
  415.5 120.4 %reduce-scatter.4.cloned.1.call-start = ((), (), s32[]{:S(2)}) async-start(), calls=%async_computation.6 | async-start | bytes 3391488
  415.5 47.7 %collective-permute-start.4 = (bf16[1440,720]{1,0:T(8,128)(2,1)}, bf16[1440,720]{1,0:T(8,128)(2,1)S(1)}, u32[]{:S(2)}, u32[]{:S(2)}) collective-permute-start(bf16[1440,720]{1,0:T(8,128)(2,1)} %param.24), channel_id=1, source_target_pairs={{0,8},{8,0},{16,24},{24,16},{32,40},{40,32},{48,56},{56,48},{64,72... | collective-permute-start | bytes 6220808 | tf_op jit(solution)/shard_map/ppermute | solution.py:25
  419.6 67.3 %collective-permute-start.5 = (bf16[360,1440]{1,0:T(8,128)(2,1)}, bf16[360,1440]{1,0:T(8,128)(2,1)}, u32[]{:S(2)}, u32[]{:S(2)}) collective-permute-start(bf16[360,1440]{1,0:T(8,128)(2,1)} %param.26), channel_id=1, source_target_pairs={{0,8},{8,0},{16,24},{24,16},{32,40},{40,32},{48,56},{56,48},{64,72... | collective-permute-start | bytes 3110408 | tf_op jit(solution)/shard_map/ppermute | solution.py:25
  448.6 14.6 %copy-start.13 = (bf16[512,1,2880]{2,0,1:T(8,128)(2,1)S(1)}, bf16[512,1,2880]{2,0,1:T(8,128)(2,1)}, u32[]{:S(2)}) copy-start(bf16[512,1,2880]{2,0,1:T(8,128)(2,1)} %all-gather.7.cloned.1.call-done) | copy-start | bytes 8847364
  537.2 17.4 %copy-start.14 = (bf16[2880,32]{0,1:T(8,128)(2,1)S(1)}, bf16[2880,32]{0,1:T(8,128)(2,1)}, u32[]{:S(2)}) copy-start(bf16[2880,32]{0,1:T(8,128)(2,1)} %param.22) | copy-start | bytes 552964
  537.2 17.6 %copy-start.7 = (s32[8,4]{0,1:T(4,128)S(1)}, s32[8,4]{0,1:T(4,128)}, u32[]{:S(2)}) copy-start(s32[8,4]{0,1:T(4,128)} %param.23) | copy-start | bytes 388
  540.2 35.4 %all-to-all-start.1 = ((bf16[64,2,1440]{2,1,0:T(2,128)(2,1)}), bf16[64,2,1440]{2,1,0:T(2,128)(2,1)S(1)}, u32[]{:S(2)}, u32[]{:S(2)}) async-start(bf16[64,2,1440]{2,1,0:T(2,128)(2,1)} %reshape.421), calls=%async_computation.1 | async-start | bytes 786432 | tf_op jit(solution)/shard_map/all_to_all | solution.py:241
Sparse Core Ops, SparseCore 0:
  10.3 140.9 all-gather.8
  154.3 138.8 all-gather.10
  298.1 76.8 all-reduce.3
  415.6 32.9 all-gather.6
  493.2 42.5 reduce-scatter.3
where the time goes:
time: 591 us; the launch traced here: 585 us
  waiting for transfers between devices  324 us (55%)
  blocking collectives  166 us (28%)
  starting transfers between devices  33.2 us (6%)
  local copies, waits for them, and re-layouts  21.5 us (4%)
  matrix products  16 us (3%)
  between operations  15.1 us (3%)
  other arithmetic  9.08 us (2%)
    all_gather x1, waiting for transfers between devices, per_device(): out_full = lax.all_gather(w_out, 'dp', axis=1, tiled=True)  129 us
    unnamed x7, waiting for transfers between devices  120 us
    all_gather x1, blocking collectives, per_device(): lax.all_gather(w_keyval, 'dp', axis=0, tiled=True)  84.7 us
    all_gather x1, blocking collectives, per_device(): lax.all_gather(attn_in, 'inner', axis=0, tiled=True)  37.2 us
    all_to_all x1, blocking collectives, per_device(): lax.all_to_all(outgoing, 'dp', split_axis=0, concat_axis=0, tiled=True)  35.9 us
    ppermute x2, waiting for transfers between devices, from_partner(): return lax.ppermute(value, axis, pairs)  28.6 us
    all_gather x1, waiting for transfers between devices, per_device(): expert_rows = lax.all_gather(received, 'inner', axis=0, tiled=True)  26.1 us
    all_to_all x1, waiting for transfers between devices, per_device(): lax.all_to_all(summed.reshape(dp_count, -1, summed.shape[-1]).astype(jnp....  20.3 us
  transfers between devices with their start and end apart: 12, of which 7 were waited for; matrix products, arithmetic and copies ran while one was open for 4% of the time, Pallas kernels for 0%

commit v1 on v0

v1 whole, which is shorter than its diff:
```python
import functools
import jax
import jax.numpy as jnp
from jax import lax
from jax.experimental import pallas as pl
from jax.experimental.pallas import tpu as pltpu
from jax.sharding import PartitionSpec as P

HEAD_DIM = 64
WINDOW = 128
MESH = pl.DeviceIdType.MESH

EPSILON = 1e-05
ROPE_BASE = 150000.0
CLAMP_LIMIT = 7.0
GLU_SLOPE = 1.702

NX = 4
NZ = 16
NI = 8
NDP = NX * NZ
ROWS = 8
GROUP = ROWS * NI
KPART = 45
KPAD = 48
QUART = NZ * KPAD
HEADS_HERE = 8
QCOLS = HEADS_HERE * HEAD_DIM
KVCOLS = 2 * HEAD_DIM
D = NX * NZ * KPART


def attention_kernel(
    tok_ref,
    gain_ref,
    seg_ref,
    wqkv_ref,
    wout_ref,
    cos_ref,
    sin_ref,
    sink_ref,
    res_ref,
    norm,
    wide,
    quarter,
    rows_in,
    wq_all,
    wo_all,
    part_f,
    part_out,
    part_in,
    seg_f,
    keyval,
    attended,
    out_part,
    out_in,
    ring_send,
    ring_recv,
    row_send,
    row_recv,
    part_send,
    part_recv,
    key_send,
    key_recv,
    att_send,
    att_recv,
    out_send,
    out_recv,
):
    dp = lax.axis_index("dp")
    inner = lax.axis_index("inner")
    x = dp // NZ
    z = dp % NZ
    right = x * NZ + (z + 1) % NZ
    left = x * NZ + (z + NZ - 1) % NZ

    barrier = pltpu.get_barrier_semaphore()

    def greet(index, carry):
        other_dp = ((x + index // NI) % NX) * NZ + z
        other_in = (inner + index % NI) % NI
        pl.semaphore_signal(barrier, inc=1, device_id=(other_dp, other_in), device_id_type=MESH)
        return carry

    lax.fori_loop(1, NX * NI, greet, 0)
    for other in (
        right,
        left,
        (dp + 1) % NDP,
        (dp + NDP - 1) % NDP,
        (dp + 2) % NDP,
        (dp + NDP - 2) % NDP,
    ):
        pl.semaphore_signal(barrier, inc=1, device_id=(other, inner), device_id_type=MESH)

    wq_all[z] = wqkv_ref[...]
    wo_all[z] = wout_ref[...]
    pl.semaphore_wait(barrier, NX * NI - 1 + 6)

    def ring(buffer, lane, step, towards, to):
        owner = (z + NZ - towards * (step - 1)) % NZ
        return pltpu.make_async_remote_copy(
            src_ref=buffer.at[owner],
            dst_ref=buffer.at[owner],
            send_sem=ring_send.at[lane, step - 1],
            recv_sem=ring_recv.at[lane, step - 1],
            device_id=(to, inner),
            device_id_type=MESH,
        )

    lanes = (
        (wq_all, 0, 1, right, 8),
        (wq_all, 1, -1, left, 7),
        (wo_all, 2, 1, right, 7),
        (wo_all, 3, -1, left, 8),
    )
    for buffer, lane, towards, to, last in lanes:
        ring(buffer, lane, 1, towards, to).start()

    values = tok_ref[...].astype(jnp.float32)
    mean_square = jnp.mean(values * values, axis=-1, keepdims=True)
    norm[...] = values * lax.rsqrt(mean_square + EPSILON) * gain_ref[...]
    wide[...] = jnp.zeros_like(wide)
    for block in range(NX * NZ):
        wide[:, block * KPAD : block * KPAD + KPART] = norm[:, block * KPART : (block + 1) * KPART]
    for part in range(NX):
        wide[:, part * QUART + KPART : part * QUART + KPART + 1] = seg_ref[...]
    for part in range(NX):
        quarter[part] = wide[:, part * QUART : (part + 1) * QUART].astype(jnp.bfloat16)

    def row_copy(index):
        other_x = (x + index // NI) % NX
        other_in = (inner + index % NI) % NI
        return pltpu.make_async_remote_copy(
            src_ref=quarter.at[other_x],
            dst_ref=rows_in.at[x * NI + inner],
            send_sem=row_send.at[index],
            recv_sem=row_recv.at[index],
            device_id=(other_x * NZ + z, other_in),
            device_id_type=MESH,
        )

    def start_row(index, carry):
        row_copy(index).start()
        return carry

    lax.fori_loop(1, NX * NI, start_row, 0)
    rows_in[x * NI + inner] = quarter[x]

    for step in range(1, 9):
        for buffer, lane, towards, to, last in lanes:
            if step <= last:
                ring(buffer, lane, step, towards, to).wait_recv()
            if step + 1 <= last:
                ring(buffer, lane, step + 1, towards, to).start()

    def wait_row(index, carry):
        row_copy(index).wait_recv()
        return carry

    lax.fori_loop(1, NX * NI, wait_row, 0)

    all_rows = rows_in[...].astype(jnp.float32).reshape(NX * GROUP, QUART)
    seg_f[...] = all_rows[:, :128].reshape(NX, GROUP, 128)
    product = jnp.dot(
        all_rows.astype(jnp.bfloat16),
        wq_all[...].reshape(QUART, QCOLS + KVCOLS),
        preferred_element_type=jnp.float32,
    ).reshape(NX, GROUP, QCOLS + KVCOLS)
    part_f[...] = product
    part_out[...] = product.astype(jnp.bfloat16)

    def part_copy(ahead):
        other = (x + ahead) % NX
        return pltpu.make_async_remote_copy(
            src_ref=part_out.at[other],
            dst_ref=part_in.at[ahead - 1],
            send_sem=part_send.at[ahead - 1],
            recv_sem=part_recv.at[ahead - 1],
            device_id=(other * NZ + z, inner),
            device_id_type=MESH,
        )

    for ahead in range(1, NX):
        part_copy(ahead).start()
    total = part_f[x]
    for ahead in range(1, NX):
        part_copy(ahead).wait_recv()
        total = total + part_in[ahead - 1].astype(jnp.float32)

    width = QCOLS + KVCOLS
    cosine = jnp.concatenate([cos_ref[:, :128]] * 4 + [cos_ref[:, 128:]], axis=1)
    sine = jnp.concatenate([sin_ref[:, :128]] * 4 + [sin_ref[:, 128:]], axis=1)
    column = lax.broadcasted_iota(jnp.int32, (GROUP, width), 1)
    swapped = jnp.where(
        column % HEAD_DIM < HEAD_DIM // 2,
        pltpu.roll(total, width - HEAD_DIM // 2, 1),
        pltpu.roll(total, HEAD_DIM // 2, 1),
    )
    turned = (total * cosine + swapped * sine).astype(jnp.bfloat16)
    own_seg = seg_f[x][:, KPART : KPART + 1]
    keyval[2, :, :KVCOLS] = turned[:, QCOLS:]
    keyval[2, :, KVCOLS:] = jnp.broadcast_to(own_seg, (GROUP, 128)).astype(jnp.bfloat16)

    def key_copy(ahead):
        return pltpu.make_async_remote_copy(
            src_ref=keyval.at[2],
            dst_ref=keyval.at[2 - ahead],
            send_sem=key_send.at[ahead - 1],
            recv_sem=key_recv.at[ahead - 1],
            device_id=((dp + ahead) % NDP, inner),
            device_id_type=MESH,
        )

    for ahead in (1, 2):
        key_copy(ahead).start()
    for ahead in (1, 2):
        key_copy(ahead).wait_recv()

    count = 3 * GROUP
    window = keyval[...].reshape(count, KVCOLS + 128)
    key_block = window[:, :HEAD_DIM]
    value_block = window[:, HEAD_DIM:KVCOLS]
    nt = (((1,), (1,)), ((), ()))
    key_seg = lax.dot_general(
        jnp.ones((GROUP, 128), jnp.bfloat16),
        window[:, KVCOLS:],
        nt,
        preferred_element_type=jnp.float32,
    )
    row = lax.broadcasted_iota(jnp.int32, (GROUP, count), 0)
    key = lax.broadcasted_iota(jnp.int32, (GROUP, count), 1)
    distance = row + 2 * GROUP - key
    allowed = (
        (distance >= 0)
        & (distance < WINDOW)
        & (key + (dp - 2) * GROUP >= 0)
        & (key_seg == own_seg * 128.0)
    )
    for head in range(HEADS_HERE):
        scores = lax.dot_general(
            turned[:, head * HEAD_DIM : (head + 1) * HEAD_DIM],
            key_block,
            nt,
            preferred_element_type=jnp.float32,
        ) * HEAD_DIM ** (-0.5)
        scores = jnp.where(allowed, scores, -1e30)
        sink = sink_ref[head]
        row_max = jnp.maximum(jnp.max(scores, axis=-1, keepdims=True), sink)
        weights = jnp.exp(scores - row_max)
        denominator = jnp.sum(weights, axis=-1, keepdims=True) + jnp.exp(sink - row_max)
        probabilities = (weights / denominator).astype(jnp.bfloat16)
        mixed = jnp.dot(probabilities, value_block, preferred_element_type=jnp.float32)
        attended[x, :, head * HEAD_DIM : (head + 1) * HEAD_DIM] = mixed.astype(jnp.bfloat16)

    def att_copy(ahead):
        return pltpu.make_async_remote_copy(
            src_ref=attended.at[x],
            dst_ref=attended.at[x],
            send_sem=att_send.at[ahead - 1],
            recv_sem=att_recv.at[ahead - 1],
            device_id=(((x + ahead) % NX) * NZ + z, inner),
            device_id_type=MESH,
        )

    for ahead in range(1, NX):
        att_copy(ahead).start()
    for ahead in range(1, NX):
        att_copy(ahead).wait_recv()
    projected = lax.dot_general(
        attended[...].reshape(NX * GROUP, QCOLS),
        wo_all[...].reshape(QUART, QCOLS),
        nt,
        preferred_element_type=jnp.float32,
    )
    out_part[...] = projected.reshape(NX * NI, ROWS, QUART).astype(jnp.bfloat16)

    def out_copy(index):
        other_x = (x + index // NI) % NX
        other_in = (inner + index % NI) % NI
        return pltpu.make_async_remote_copy(
            src_ref=out_part.at[other_x * NI + other_in],
            dst_ref=out_in.at[x * NI + inner],
            send_sem=out_send.at[index],
            recv_sem=out_recv.at[index],
            device_id=(other_x * NZ + z, other_in),
            device_id_type=MESH,
        )

    def start_out(index, carry):
        out_copy(index).start()
        return carry

    def wait_out(index, carry):
        out_copy(index).wait_recv()
        return carry

    lax.fori_loop(1, NX * NI, start_out, 0)
    out_in[x * NI + inner] = out_part[x * NI + inner]
    lax.fori_loop(1, NX * NI, wait_out, 0)
    summed = jnp.sum(
        out_in[...].astype(jnp.float32).reshape(NX, NI, ROWS, QUART), axis=1
    )
    for part in range(NX):
        wide[:, part * QUART : (part + 1) * QUART] = summed[part]
    for block in range(NX * NZ):
        norm[:, block * KPART : (block + 1) * KPART] = wide[:, block * KPAD : block * KPAD + KPART]
    res_ref[...] = (tok_ref[...].astype(jnp.float32) + norm[...]).astype(jnp.bfloat16)

    for buffer, lane, towards, to, last in lanes:
        for step in range(1, last + 1):
            ring(buffer, lane, step, towards, to).wait_send()

    def wait_sends(index, carry):
        row_copy(index).wait_send()
        out_copy(index).wait_send()
        return carry

    lax.fori_loop(1, NX * NI, wait_sends, 0)
    for ahead in range(1, NX):
        part_copy(ahead).wait_send()
        att_copy(ahead).wait_send()
    for ahead in (1, 2):
        key_copy(ahead).wait_send()


def rope_tables(dp_index):
    half = HEAD_DIM // 2
    frequency = ROPE_BASE ** (-2.0 * jnp.arange(half, dtype=jnp.float32) / HEAD_DIM)
    positions = dp_index * GROUP + jnp.arange(GROUP, dtype=jnp.int32)
    angles = positions.astype(jnp.float32)[:, None] * frequency[None, :]
    cosine = jnp.cos(angles)
    sine = jnp.sin(angles)
    ones = jnp.ones((GROUP, HEAD_DIM), jnp.float32)
    head_cos = jnp.concatenate([cosine, cosine], axis=1)
    head_sin = jnp.concatenate([-sine, sine], axis=1)
    return (
        jnp.concatenate([head_cos, head_cos, head_cos, ones], axis=1),
        jnp.concatenate([head_sin, head_sin, head_sin, 0.0 * ones], axis=1),
    )


def attention_layer(tokens, segments, attn_gain, w_query, w_keyval, sink_logits, w_out):
    dp_index = lax.axis_index("dp")
    cos_table, sin_table = rope_tables(dp_index)
    pad_rows = ((0, KPAD - KPART), (0, 0))
    w_in = jnp.pad(jnp.concatenate([w_query, w_keyval], axis=1), pad_rows)
    w_back = jnp.pad(w_out.T, pad_rows)
    vmem = pl.BlockSpec(memory_space=pltpu.VMEM)
    width = QCOLS + KVCOLS
    bf16, f32 = jnp.bfloat16, jnp.float32
    dma = pltpu.SemaphoreType.DMA
    return pl.pallas_call(
        attention_kernel,
        out_shape=jax.ShapeDtypeStruct((ROWS, D), bf16),
        in_specs=[vmem] * 7 + [pl.BlockSpec(memory_space=pltpu.SMEM)],
        out_specs=vmem,
        scratch_shapes=[
            pltpu.VMEM((ROWS, D), f32),
            pltpu.VMEM((ROWS, NX * QUART), f32),
            pltpu.VMEM((NX, ROWS, QUART), bf16),
            pltpu.VMEM((NX * NI, ROWS, QUART), bf16),
            pltpu.VMEM((NZ, KPAD, width), bf16),
            pltpu.VMEM((NZ, KPAD, QCOLS), bf16),
            pltpu.VMEM((NX, GROUP, width), f32),
            pltpu.VMEM((NX, GROUP, width), bf16),
            pltpu.VMEM((NX - 1, GROUP, width), bf16),
            pltpu.VMEM((NX, GROUP, 128), f32),
            pltpu.VMEM((3, GROUP, KVCOLS + 128), bf16),
            pltpu.VMEM((NX, GROUP, QCOLS), bf16),
            pltpu.VMEM((NX * NI, ROWS, QUART), bf16),
            pltpu.VMEM((NX * NI, ROWS, QUART), bf16),
            dma((4, 8)),
            dma((4, 8)),
            dma((NX * NI,)),
            dma((NX * NI,)),
            dma((NX - 1,)),
            dma((NX - 1,)),
            dma((2,)),
            dma((2,)),
            dma((NX - 1,)),
            dma((NX - 1,)),
            dma((NX * NI,)),
            dma((NX * NI,)),
        ],
        compiler_params=pltpu.CompilerParams(
            collective_id=0, has_side_effects=True, vmem_limit_bytes=48 * 2**20
        ),
        name="attention",
    )(
        tokens,
        attn_gain.reshape(1, D),
        segments.astype(f32).reshape(ROWS, 1),
        w_in,
        w_back,
        cos_table,
        sin_table,
        sink_logits,
    )


def from_partner(value, axis, apart):
    mask = 2**apart
    pairs = [(source, source ^ mask) for source in range(lax.axis_size(axis))]
    return lax.ppermute(value, axis, pairs)


def rms_scale(row_block, gain_vector):
    values = row_block.astype(jnp.float32)
    mean_square = jnp.mean(values * values, axis=-1, keepdims=True)
    return (values * lax.rsqrt(mean_square + EPSILON) * gain_vector).astype(jnp.bfloat16)


def slot_numbers(route_block, expert_count):
    flat_routes = route_block.reshape(-1)
    onehot = (flat_routes[:, None] == jnp.arange(expert_count, dtype=jnp.int32)[None, :]).astype(
        jnp.int32
    )
    earlier = jnp.cumsum(onehot, axis=0) - onehot
    return jnp.sum(earlier * onehot, axis=1).reshape(route_block.shape)


def route_mix(moe_rows, w_router, route_block):
    expert_count = w_router.shape[1]
    logits = jnp.dot(moe_rows, w_router, preferred_element_type=jnp.float32)
    matches = route_block[:, :, None] == jnp.arange(expert_count, dtype=jnp.int32)[None, None, :]
    chosen = jnp.sum(jnp.where(matches, logits[:, None, :], 0.0), axis=-1)
    return (jax.nn.softmax(chosen, axis=-1), matches)


def send_table(targets, length):
    columns = jnp.arange(length, dtype=jnp.int32)
    return jnp.any(columns[:, None, None] == targets[None, :, :], axis=-1).astype(jnp.bfloat16)


def spread_rows(table, row_block, dp_count):
    placed = jnp.dot(table, row_block, preferred_element_type=jnp.float32)
    return placed.astype(jnp.bfloat16).reshape(dp_count, -1, row_block.shape[1])


def join_rows(returned):
    dp_count, span, width = returned.shape
    return returned.reshape(-1, width)


def pick_rows(returned, targets, weights):
    taken = jnp.take(returned, targets, axis=0).astype(jnp.float32)
    return jnp.sum(weights[:, :, None] * taken, axis=1)


def activate(gate_up):
    gate_part = jnp.minimum(gate_up[:, 0::2], CLAMP_LIMIT)
    up_part = jnp.clip(gate_up[:, 1::2], -CLAMP_LIMIT, CLAMP_LIMIT)
    return ((up_part + 1.0) * gate_part * jax.nn.sigmoid(GLU_SLOPE * gate_part)).astype(
        jnp.bfloat16
    )


def per_device(
    tokens,
    segments,
    attn_gain,
    w_query,
    w_keyval,
    sink_logits,
    w_out,
    moe_gain,
    w_router,
    routes,
    w_gate_up,
    b_gate_up,
    w_down,
    b_down,
):
    tok_rows, model_width = tokens.shape
    dp_count = lax.axis_size("dp")
    dp_index = lax.axis_index("dp")
    inner_index = lax.axis_index("inner")
    residual = attention_layer(
        tokens, segments, attn_gain, w_query, w_keyval, sink_logits, w_out
    )
    moe_in = rms_scale(residual, moe_gain)
    expert_count = w_router.shape[1]
    capacity = 16 * tok_rows // dp_count
    half_cap = capacity // 2
    parity = dp_index % 2
    expert_id = dp_index // 2
    half_rows = w_gate_up.shape[0]
    bias_row = lax.dynamic_slice_in_dim(b_gate_up, expert_id, 1, 0)
    gate_other, down_other = from_partner((w_gate_up, w_down), "dp", 0)
    mix, matches = route_mix(moe_in, w_router, routes)
    expert_mix = jnp.sum(jnp.where(matches, mix[:, :, None], 0.0), axis=1)
    bias_term = jnp.dot(expert_mix, b_down, precision=lax.Precision.HIGHEST)
    slot_index = slot_numbers(routes, expert_count)
    source_flip = (dp_index + inner_index) % 2
    slot_half = (slot_index // half_cap + source_flip) % 2
    targets = routes * capacity + slot_half * half_cap + slot_index % half_cap
    length = expert_count * capacity
    outgoing = spread_rows(send_table(targets, length), moe_in, dp_count)
    received = lax.all_to_all(outgoing, "dp", split_axis=0, concat_axis=0, tiled=True)
    expert_rows = lax.all_gather(received, "inner", axis=0, tiled=True)
    row_block = expert_rows.reshape(-1, expert_rows.shape[-1])
    own_cols = lax.dynamic_slice_in_dim(row_block, parity * half_rows, half_rows, 1)
    other_cols = lax.dynamic_slice_in_dim(row_block, (1 - parity) * half_rows, half_rows, 1)
    own_part = jnp.dot(own_cols, w_gate_up, preferred_element_type=jnp.float32).astype(jnp.bfloat16)
    other_part = jnp.dot(other_cols, gate_other, preferred_element_type=jnp.float32).astype(
        jnp.bfloat16
    )
    own_part, other_part = lax.optimization_barrier((own_part, other_part))
    hidden = activate(own_part.astype(jnp.float32) + other_part.astype(jnp.float32) + bias_row)
    own_out = jnp.dot(hidden, w_down, preferred_element_type=jnp.float32)
    other_out = jnp.dot(hidden, down_other, preferred_element_type=jnp.float32)
    joined = jnp.where(
        parity == 0,
        jnp.concatenate([own_out, other_out], axis=1),
        jnp.concatenate([other_out, own_out], axis=1),
    )
    partial_value = joined.astype(jnp.bfloat16)
    summed = lax.psum_scatter(partial_value, "inner", scatter_dimension=0, tiled=True).astype(
        jnp.float32
    )
    returned = lax.all_to_all(
        summed.reshape(dp_count, -1, summed.shape[-1]).astype(jnp.bfloat16),
        "dp",
        split_axis=0,
        concat_axis=0,
        tiled=True,
    ).astype(jnp.float32)
    moe_sum = pick_rows(join_rows(returned), targets, mix)
    return (residual.astype(jnp.float32) + moe_sum + bias_term).astype(jnp.bfloat16)


def solution(mesh):
    return jax.shard_map(
        per_device,
        mesh=mesh,
        in_specs=(
            P(("dp", "inner"), None),
            P(("dp", "inner")),
            P(),
            P("dp", "inner"),
            P("dp", "inner"),
            P("inner"),
            P("inner", "dp"),
            P(),
            P(),
            P(("dp", "inner"), None),
            P("dp", "inner"),
            P(None, "inner"),
            P("inner", "dp"),
            P(),
        ),
        out_specs=P(("dp", "inner"), None),
        check_vma=False,
    )
```

time: 591 us -> 296 us (0.50)
  the two profiles are of different devices: /device:TPU:1 before, /device:TPU:31 now
where the time goes in v1:
time: 296 us; the launch traced here: 295 us
  waiting for transfers between devices  119 us (40%)
  Pallas kernels  71.7 us (24%)
  blocking collectives  34 us (11%)
  starting transfers between devices  21.7 us (7%)
  local copies, waits for them, and re-layouts  16.3 us (6%)
  between operations  13.7 us (5%)
  matrix products  12.1 us (4%)
  other arithmetic  6.59 us (2%)
    pallas_call x1, Pallas kernels, attention_layer(): pl.pallas_call(attention_kernel, out_shape=jax.ShapeDtypeStruct((ROWS, D)...  71.7 us
    ppermute x2, waiting for transfers between devices, from_partner(): return lax.ppermute(value, axis, pairs)  36.9 us
    unnamed x3, waiting for transfers between devices  35.8 us
    all_to_all x1, blocking collectives, per_device(): lax.all_to_all(outgoing, 'dp', split_axis=0, concat_axis=0, tiled=True)  34 us
    all_to_all x1, waiting for transfers between devices, per_device(): lax.all_to_all(summed.reshape(dp_count, -1, summed.shape[-1]).astype(jnp....  25.5 us
    all_gather x1, waiting for transfers between devices, per_device(): expert_rows = lax.all_gather(received, 'inner', axis=0, tiled=True)  21.1 us
    all_to_all x1, starting transfers between devices, per_device(): lax.all_to_all(summed.reshape(dp_count, -1, summed.shape[-1]).astype(jnp....  15.4 us
    unnamed x22, local copies, waits for them, and re-layouts  9.72 us
  transfers between devices with their start and end apart: 5, of which 5 were waited for; matrix products, arithmetic and copies ran while one was open for 4% of the time, Pallas kernels for 0%

profile of v1, /device:TPU:31, one launch (start us, length us, event | category | flops | bytes accessed | tf_op | source)
XLA Modules:
  0.0 295.4 jit_solution(16203335642741955679)
XLA Ops:
  6.6 0.8 copy.52
  8.0 0.7 reshape.86.gain_ref
  9.8 0.8 fusion.20.wqkv_ref
  10.7 0.8 pad.9.wout_ref
  11.6 0.8 copy-done.1
  13.1 71.7 %attention.1 = bf16[8,2880]{1,0:T(8,128)(2,1)S(1)} custom-call(bf16[8,2880]{1,0:T(8,128)(2,1)S(1)} %copy-done.1, f32[1,2880]{1,0:T(1,128)S(1)} %reshape.86.gain_ref, f32[8,1]{1,0:T(8,128)S(1)} %copy.50.seg_ref, bf16[48,640]{1,0:T(8,128)(2,1)S(1)} %fusion.20.wqkv_ref, bf16[48,512]{1,0:T(8,128)(2,1)S(1)} %pad.9.wout_ref, f32[64,256]{1,0:T(8,128)S(1)} %concatenate.20.cos_ref, ...), custom_call_target="tpu_custom_call" | custom-call | tf_op jit(solution)/shard_map/attention/pallas_call | solution.py:353
  84.9 1.0 fusion.1
  86.5 0.8 reduce.2
  87.8 34.0 %all_to_all.10 = bf16[64,2,1440]{2,1,0:T(2,128)(2,1)S(1)} all-to-all(bf16[64,2,1440]{2,1,0:T(2,128)(2,1)S(1)} %reshape.106), channel_id=1, replica_groups=mesh['dp'=64,'inner'=8] {'dp'}, dimensions={0} | all-to-all | bytes 737280 | tf_op jit(solution)/shard_map/all_to_all | solution.py:500
  122.3 0.8 copy.56
  123.1 4.2 %collective-permute-start = (bf16[1440,720]{1,0:T(8,128)(2,1)}, bf16[1440,720]{1,0:T(8,128)(2,1)S(1)}, u32[]{:S(2)}, u32[]{:S(2)}) collective-permute-start(bf16[1440,720]{1,0:T(8,128)(2,1)} %param.24), channel_id=1, source_target_pairs={{0,8},{8,0},{16,24},{24,16},{32,40},{40,32},{48,56},{56,48},{64,72... | collective-permute-start | bytes 6220808 | tf_op jit(solution)/shard_map/ppermute | solution.py:405
  127.4 2.1 collective-permute-start.1
  129.5 0.8 dynamic-slice_reduce_fusion
  130.3 21.1 %all-gather.2.cloned.1.call-done = bf16[512,1,2880]{2,0,1:T(8,128)(2,1)} async-done(((bf16[64,1,2880]{2,0,1:T(8,128)(2,1)}), bf16[512,1,2880]{2,0,1:T(8,128)(2,1)}) %all-gather.2.cloned.1.call-update) | async-done | bytes 2949136 | tf_op jit(solution)/shard_map/all_gather | solution.py:501
  151.4 3.9 %fusion.9 = bf16[512,720]{0,1:T(8,128)(2,1)S(1)} fusion(bf16[1440,720]{1,0:T(8,128)(2,1)} %param.24, bf16[512,1,2880]{2,0,1:T(8,128)(2,1)} %all-gather.2.cloned.1.call-done, s32[]{:T(128)S(6)} %select_n.66), kind=kOutput, calls=%fused_computation.14 | convolution fusion | flops 1062051840 | bytes 4521988 | tf_op jit(solution)/shard_map/dot_general | solution.py:505
  155.2 19.0 %collective-permute-done = bf16[1440,720]{1,0:T(8,128)(2,1)S(1)} collective-permute-done((bf16[1440,720]{1,0:T(8,128)(2,1)}, bf16[1440,720]{1,0:T(8,128)(2,1)S(1)}, u32[]{:S(2)}, u32[]{:S(2)}) %collective-permute-start) | collective-permute-done | bytes 2073632 | tf_op jit(solution)/shard_map/ppermute | solution.py:405
  174.3 1.6 fusion.12
  176.1 0.7 slice.6
  176.8 0.7 slice.7
  177.8 2.2 fusion.34
  180.1 17.9 %collective-permute-done.1 = bf16[360,1440]{1,0:T(8,128)(2,1)} collective-permute-done((bf16[360,1440]{1,0:T(8,128)(2,1)}, bf16[360,1440]{1,0:T(8,128)(2,1)}, u32[]{:S(2)}, u32[]{:S(2)}) %collective-permute-start.1) | collective-permute-done | bytes 1036832 | tf_op jit(solution)/shard_map/ppermute | solution.py:405
  198.0 2.2 fusion.35
  200.2 0.9 fusion
  201.1 3.0 %copy.61 = bf16[512,2880]{1,0:T(8,128)(2,1)} copy(bf16[512,2880]{0,1:T(8,128)(2,1)S(1)} %fusion) | data formatting | bytes 5898240
  204.1 35.7 %reduce-scatter.4.cloned.1.call-done = bf16[64,2880]{1,0:T(8,128)(2,1)} async-done(((bf16[512,2880]{1,0:T(8,128)(2,1)}), bf16[64,2880]{1,0:T(8,128)(2,1)}) %reduce-scatter.4.cloned.1.call-update) | async-done | bytes 368656
  239.9 1.4 copy.62
  241.3 1.4 reduce.3
  243.0 1.2 reshape.108
  244.2 15.4 %all-to-all-start.1 = ((bf16[64,2,1440]{2,1,0:T(2,128)(2,1)}), bf16[64,2,1440]{2,1,0:T(2,128)(2,1)S(1)}, u32[]{:S(2)}, u32[]{:S(2)}) async-start(bf16[64,2,1440]{2,1,0:T(2,128)(2,1)} %reshape.108), calls=%async_computation.1 | async-start | bytes 786432 | tf_op jit(solution)/shard_map/all_to_all | solution.py:522
  260.3 25.5 %all-to-all-done.1 = bf16[64,2,1440]{2,1,0:T(2,128)(2,1)S(1)} async-done(((bf16[64,2,1440]{2,1,0:T(2,128)(2,1)}), bf16[64,2,1440]{2,1,0:T(2,128)(2,1)S(1)}, u32[]{:S(2)}, u32[]{:S(2)}) %all-to-all-start.1) | async-done | bytes 368672 | tf_op jit(solution)/shard_map/all_to_all | solution.py:522
  286.4 0.7 gather_fusion
  287.6 0.9 fusion.2
  (57 shorter events, 6.8 us)
Async XLA Ops:
  6.5 281.1 %copy-start = (f32[32,2880]{1,0:T(8,128)S(1)}, f32[32,2880]{1,0:T(8,128)}, u32[]{:S(2)}) copy-start(f32[32,2880]{1,0:T(8,128)} %param.27) | copy-start | bytes 1105924
  6.5 144.8 %all-gather.2.cloned.1.call-start = ((), (), s32[]{:S(2)}) async-start(), calls=%async_computation.3 | async-start | bytes 3391488 | tf_op jit(solution)/shard_map/all_gather | solution.py:501
  11.6 0.8 copy-start.1
  12.4 0.7 copy-start.2
  123.1 116.8 %reduce-scatter.4.cloned.1.call-start = ((), (), s32[]{:S(2)}) async-start(), calls=%async_computation.4 | async-start | bytes 3391488
  123.1 51.1 %collective-permute-start = (bf16[1440,720]{1,0:T(8,128)(2,1)}, bf16[1440,720]{1,0:T(8,128)(2,1)S(1)}, u32[]{:S(2)}, u32[]{:S(2)}) collective-permute-start(bf16[1440,720]{1,0:T(8,128)(2,1)} %param.24), channel_id=1, source_target_pairs={{0,8},{8,0},{16,24},{24,16},{32,40},{40,32},{48,56},{56,48},{64,72... | collective-permute-start | bytes 6220808 | tf_op jit(solution)/shard_map/ppermute | solution.py:405
  127.4 70.6 %collective-permute-start.1 = (bf16[360,1440]{1,0:T(8,128)(2,1)}, bf16[360,1440]{1,0:T(8,128)(2,1)}, u32[]{:S(2)}, u32[]{:S(2)}) collective-permute-start(bf16[360,1440]{1,0:T(8,128)(2,1)} %param.26), channel_id=1, source_target_pairs={{0,8},{8,0},{16,24},{24,16},{32,40},{40,32},{48,56},{56,48},{64,72... | collective-permute-start | bytes 3110408 | tf_op jit(solution)/shard_map/ppermute | solution.py:405
  151.4 22.9 %copy-start.5 = (bf16[512,1,2880]{2,0,1:T(8,128)(2,1)S(1)}, bf16[512,1,2880]{2,0,1:T(8,128)(2,1)}, u32[]{:S(2)}) copy-start(bf16[512,1,2880]{2,0,1:T(8,128)(2,1)} %all-gather.2.cloned.1.call-done) | copy-start | bytes 8847364
  241.2 18.4 %copy-start.4 = (f32[2880]{0:T(1024)S(1)}, f32[2880]{0:T(1024)}, u32[]{:S(2)}) copy-start(f32[2880]{0:T(1024)} %param.21) | copy-start | bytes 34564
  241.3 18.4 %copy-start.6 = (bf16[2880,32]{0,1:T(8,128)(2,1)S(1)}, bf16[2880,32]{0,1:T(8,128)(2,1)}, u32[]{:S(2)}) copy-start(bf16[2880,32]{0,1:T(8,128)(2,1)} %param.22) | copy-start | bytes 552964
  241.3 18.6 %copy-start.3 = (s32[8,4]{0,1:T(4,128)S(1)}, s32[8,4]{0,1:T(4,128)}, u32[]{:S(2)}) copy-start(s32[8,4]{0,1:T(4,128)} %param.23) | copy-start | bytes 388
  244.2 41.6 %all-to-all-start.1 = ((bf16[64,2,1440]{2,1,0:T(2,128)(2,1)}), bf16[64,2,1440]{2,1,0:T(2,128)(2,1)S(1)}, u32[]{:S(2)}, u32[]{:S(2)}) async-start(bf16[64,2,1440]{2,1,0:T(2,128)(2,1)} %reshape.108), calls=%async_computation.1 | async-start | bytes 786432 | tf_op jit(solution)/shard_map/all_to_all | solution.py:522
Sparse Core Ops, SparseCore 0:
  123.2 28.1 all-gather.1
  204.3 35.5 reduce-scatter.3

commit v2 on v1

--- a/solution.py
+++ b/solution.py
@@ -28,9 +28,18 @@
 QCOLS = HEADS_HERE * HEAD_DIM
 KVCOLS = 2 * HEAD_DIM
 D = NX * NZ * KPART
-
-
-def attention_kernel(
+HALF = D // 2
+HPAD = 1536
+TAIL = 1408
+TABLE = HALF - TAIL
+EXPERTS = 32
+SLOTS = 2 * NX * NZ
+UNITS = 360
+UPAD = 384
+NY = 4
+
+
+def layer_kernel(
     tok_ref,
     gain_ref,
     seg_ref,
@@ -39,7 +48,14 @@
     cos_ref,
     sin_ref,
     sink_ref,
-    res_ref,
+    moe_gain_ref,
+    routes_ref,
+    router_hbm,
+    gate_hbm,
+    gate_bias_hbm,
+    down_hbm,
+    down_bias_hbm,
+    out_ref,
     norm,
     wide,
     quarter,
@@ -66,6 +82,51 @@
     att_recv,
     out_send,
     out_recv,
+    res,
+    router,
+    gate_raw,
+    gate_w,
+    gate_bias,
+    down_w,
+    down_bias,
+    load_sem,
+    halves,
+    pay,
+    gathered,
+    picked,
+    rows_all,
+    gate_own,
+    gate_in,
+    hidden,
+    sib_out,
+    sib_in,
+    pair_out,
+    pair_in,
+    sum_own,
+    back_out,
+    back_in,
+    mixed_out,
+    mixed_in,
+    z_send,
+    z_recv,
+    x_send,
+    x_recv,
+    y_send,
+    y_recv,
+    sib_send,
+    sib_recv,
+    gate_send,
+    gate_recv,
+    hid_send,
+    hid_recv,
+    fold_send,
+    fold_recv,
+    pair_send,
+    pair_recv,
+    back_send,
+    back_recv,
+    mix_send,
+    mix_recv,
 ):
     dp = lax.axis_index("dp")
     inner = lax.axis_index("inner")
@@ -83,9 +144,14 @@
         return carry
 
     lax.fori_loop(1, NX * NI, greet, 0)
+
+    def greet_z(index, carry):
+        other = x * NZ + (z + index) % NZ
+        pl.semaphore_signal(barrier, inc=1, device_id=(other, inner), device_id_type=MESH)
+        return carry
+
+    lax.fori_loop(1, NZ, greet_z, 0)
     for other in (
-        right,
-        left,
         (dp + 1) % NDP,
         (dp + NDP - 1) % NDP,
         (dp + 2) % NDP,
@@ -93,9 +159,23 @@
     ):
         pl.semaphore_signal(barrier, inc=1, device_id=(other, inner), device_id_type=MESH)
 
+    loads = [
+        pltpu.make_async_copy(source, target, load_sem.at[number])
+        for number, (source, target) in enumerate(
+            (
+                (router_hbm, router),
+                (gate_hbm, gate_raw),
+                (gate_bias_hbm, gate_bias),
+                (down_hbm, down_w),
+                (down_bias_hbm, down_bias),
+            )
+        )
+    ]
+    for load in loads:
+        load.start()
     wq_all[z] = wqkv_ref[...]
     wo_all[z] = wout_ref[...]
-    pl.semaphore_wait(barrier, NX * NI - 1 + 6)
+    pl.semaphore_wait(barrier, NX * NI - 1 + NZ - 1 + 4)
 
     def ring(buffer, lane, step, towards, to):
         owner = (z + NZ - towards * (step - 1)) % NZ
@@ -305,7 +385,361 @@
         wide[:, part * QUART : (part + 1) * QUART] = summed[part]
     for block in range(NX * NZ):
         norm[:, block * KPART : (block + 1) * KPART] = wide[:, block * KPAD : block * KPAD + KPART]
-    res_ref[...] = (tok_ref[...].astype(jnp.float32) + norm[...]).astype(jnp.bfloat16)
+    res[...] = (tok_ref[...].astype(jnp.float32) + norm[...]).astype(jnp.bfloat16)
+
+    bf16, f32 = jnp.bfloat16, jnp.float32
+    nn = (((1,), (0,)), ((), ()))
+
+    def iota(shape, dimension):
+        return lax.broadcasted_iota(jnp.int32, shape, dimension)
+
+    def ones_where(condition):
+        return jnp.where(condition, 1.0, 0.0)
+
+    half = z % 2
+    chip_y = inner // 2
+    core = inner % 2
+    partner = x * NZ + z + 1 - 2 * half
+    sibling = inner + 1 - 2 * core
+    for load in loads:
+        load.wait()
+
+    values = res[...].astype(f32)
+    mean_square = jnp.mean(values * values, axis=-1, keepdims=True)
+    moe_in = (values * lax.rsqrt(mean_square + EPSILON) * moe_gain_ref[...]).astype(bf16)
+    norm[...] = moe_in.astype(f32)
+    halves[...] = jnp.zeros_like(halves)
+    for part in range(2):
+        halves[part, :, :HALF] = norm[:, part * HALF : (part + 1) * HALF]
+
+    logits = jnp.dot(moe_in, router[...], preferred_element_type=f32)
+    expert = iota((ROWS, EXPERTS), 1)
+    named = [ones_where(routes_ref[:, k : k + 1] == expert) for k in range(4)]
+    chosen = [jnp.sum(match * logits, axis=-1, keepdims=True) for match in named]
+    largest = jnp.maximum(jnp.maximum(chosen[0], chosen[1]), jnp.maximum(chosen[2], chosen[3]))
+    raised = [jnp.exp(value - largest) for value in chosen]
+    whole = raised[0] + raised[1] + raised[2] + raised[3]
+    onehot = named[0] + named[1] + named[2] + named[3]
+    mix = (
+        named[0] * raised[0] + named[1] * raised[1] + named[2] * raised[2] + named[3] * raised[3]
+    ) / whole
+    earlier = jnp.dot(
+        ones_where(iota((ROWS, ROWS), 0) > iota((ROWS, ROWS), 1)),
+        onehot,
+        preferred_element_type=f32,
+    )
+    mix_high = mix.astype(bf16).astype(f32)
+    mix_low = mix - mix_high
+    column = iota((EXPERTS, 8 * 128), 1)
+    source = iota((EXPERTS, 8 * 128), 0)
+    table = jnp.zeros((ROWS, 8 * 128), f32)
+    for slot in range(2):
+        here = onehot * ones_where(earlier == slot)
+        for kind, value in enumerate((here, here * mix_high, here * mix_low)):
+            place = (source % 8) * 128 + TABLE + kind * 8 + (source // 8) * 2 + slot
+            table = table + jnp.dot(
+                value.astype(bf16),
+                ones_where(column == place).astype(bf16),
+                preferred_element_type=f32,
+            )
+    for other in range(NZ):
+        part = other % 2
+        pair = other // 2
+        pay[other, :, :TAIL] = halves[part, :, :TAIL].astype(bf16)
+        pay[other, :, TAIL:] = (
+            halves[part, :, TAIL:] + table[:, pair * 128 : (pair + 1) * 128]
+        ).astype(bf16)
+
+    def z_copy(index):
+        other = (z + index) % NZ
+        return pltpu.make_async_remote_copy(
+            src_ref=pay.at[other],
+            dst_ref=gathered.at[z],
+            send_sem=z_send.at[index],
+            recv_sem=z_recv.at[index],
+            device_id=(x * NZ + other, inner),
+            device_id_type=MESH,
+        )
+
+    def start_z(index, carry):
+        z_copy(index).start()
+        return carry
+
+    def wait_z(index, carry):
+        z_copy(index).wait_recv()
+        return carry
+
+    lax.fori_loop(1, NZ, start_z, 0)
+    gathered[z] = pay[z]
+
+    bias_term = jnp.dot(mix, down_bias[...], precision=lax.Precision.HIGHEST)
+    target = iota((2 * UNITS, 2 * UPAD), 1)
+    place = iota((2 * UNITS, 2 * UPAD), 0)
+    unweave = ones_where(target == place // 2 + (place % 2) * UPAD).astype(bf16)
+
+    def sort_columns(index, carry):
+        lines = pl.ds(pl.multiple_of(index * 144, 16), 144)
+        gate_w[lines, :] = jnp.dot(gate_raw[lines, :], unweave, preferred_element_type=f32).astype(
+            bf16
+        )
+        return carry
+
+    lax.fori_loop(0, HALF // 144, sort_columns, 0)
+    bias_row = gate_bias[pl.ds(dp // 2, 1), :]
+    bias_high = bias_row.astype(bf16).astype(f32)
+    bias_mid = (bias_row - bias_high).astype(bf16).astype(f32)
+    bias_low = bias_row - bias_high - bias_mid
+    line = iota((ROWS, 2 * UNITS), 0)
+    bias_parts = jnp.where(
+        line == 0, bias_high, jnp.where(line == 1, bias_mid, jnp.where(line == 2, bias_low, 0.0))
+    )
+    bias = jnp.sum(
+        jnp.dot(bias_parts.astype(bf16), unweave, preferred_element_type=f32),
+        axis=0,
+        keepdims=True,
+    )
+
+    lax.fori_loop(1, NZ, wait_z, 0)
+    row_total = NZ * ROWS
+    near = gathered[...].astype(f32).reshape(row_total, HPAD)
+    near_tail = near[:, TAIL:].astype(bf16)
+    slot_row = iota((SLOTS, 128), 0)
+    slot_lane = iota((SLOTS, 128), 1)
+    select = lax.dot_general(
+        ones_where(slot_lane - TABLE == slot_row // NZ).astype(bf16),
+        near_tail,
+        nt,
+        preferred_element_type=f32,
+    ) * ones_where(slot_row % NZ == slot_lane // ROWS)
+    chosen_rows = jnp.dot(
+        select.astype(bf16), near[:, :HALF].astype(bf16), preferred_element_type=f32
+    )
+    picked[...] = chosen_rows.astype(bf16).reshape(NX, 2 * NZ, HALF)
+
+    def mix_matrix(kind):
+        spread = jnp.dot(
+            near_tail,
+            ones_where(slot_row - TABLE - kind * 8 == slot_lane // NZ).astype(bf16),
+            preferred_element_type=f32,
+        )
+        return (spread * ones_where(slot_row // ROWS == slot_lane % NZ)).astype(bf16)
+
+    def x_copy(ahead):
+        other = (x + ahead) % NX
+        return pltpu.make_async_remote_copy(
+            src_ref=picked.at[other],
+            dst_ref=rows_all.at[inner, x],
+            send_sem=x_send.at[ahead],
+            recv_sem=x_recv.at[ahead],
+            device_id=(other * NZ + z, inner),
+            device_id_type=MESH,
+        )
+
+    def y_copy(ahead, back):
+        block = rows_all.at[inner, (x + NX - back) % NX]
+        return pltpu.make_async_remote_copy(
+            src_ref=block,
+            dst_ref=block,
+            send_sem=y_send.at[ahead, back],
+            recv_sem=y_recv.at[ahead, back],
+            device_id=(dp, ((chip_y + ahead) % NY) * 2 + core),
+            device_id_type=MESH,
+        )
+
+    def sib_copy(turn, chip):
+        chunk = rows_all.at[chip * 2 + core]
+        return pltpu.make_async_remote_copy(
+            src_ref=chunk,
+            dst_ref=chunk,
+            send_sem=sib_send.at[turn],
+            recv_sem=sib_recv.at[turn],
+            device_id=(dp, sibling),
+            device_id_type=MESH,
+        )
+
+    for ahead in range(1, NX):
+        x_copy(ahead).start()
+    rows_all[inner, x] = picked[x]
+    for back in range(NX):
+        if back:
+            x_copy(back).wait_recv()
+        for ahead in (1, 3, 2):
+            y_copy(ahead, back).start()
+    sib_copy(0, chip_y).start()
+
+    def gate_copy(chunk):
+        return pltpu.make_async_remote_copy(
+            src_ref=gate_own.at[chunk, 1 - half],
+            dst_ref=gate_in.at[chunk],
+            send_sem=gate_send.at[chunk],
+            recv_sem=gate_recv.at[chunk],
+            device_id=(partner, inner),
+            device_id_type=MESH,
+        )
+
+    def hid_copy(chunk):
+        return pltpu.make_async_remote_copy(
+            src_ref=hidden.at[chunk, half],
+            dst_ref=hidden.at[chunk, half],
+            send_sem=hid_send.at[chunk],
+            recv_sem=hid_recv.at[chunk],
+            device_id=(partner, inner),
+            device_id_type=MESH,
+        )
+
+    def fold_copy(turn):
+        return pltpu.make_async_remote_copy(
+            src_ref=sib_out.at[turn],
+            dst_ref=sib_in.at[turn],
+            send_sem=fold_send.at[turn],
+            recv_sem=fold_recv.at[turn],
+            device_id=(dp, sibling),
+            device_id_type=MESH,
+        )
+
+    def pair_copy(turn, back):
+        return pltpu.make_async_remote_copy(
+            src_ref=pair_out.at[turn],
+            dst_ref=pair_in.at[turn],
+            send_sem=pair_send.at[turn],
+            recv_sem=pair_recv.at[turn],
+            device_id=(dp, ((chip_y + NY - back) % NY) * 2 + core),
+            device_id_type=MESH,
+        )
+
+    def project(chunk):
+        rows = rows_all[chunk].reshape(SLOTS, HALF)
+        gate_own[chunk] = (
+            jnp.dot(rows, gate_w[...], preferred_element_type=f32)
+            .astype(bf16)
+            .reshape(2, SLOTS // 2, 2 * UPAD)
+        )
+        gate_copy(chunk).start()
+
+    def activate(chunk):
+        gate_copy(chunk).wait_recv()
+        gate_up = gate_own[chunk, half].astype(f32) + gate_in[chunk].astype(f32) + bias
+        gate = jnp.minimum(gate_up[:, :UPAD], CLAMP_LIMIT)
+        up = jnp.clip(gate_up[:, UPAD:], -CLAMP_LIMIT, CLAMP_LIMIT)
+        hidden[chunk, half] = ((up + 1.0) * gate * jax.nn.sigmoid(GLU_SLOPE * gate)).astype(bf16)
+        hid_copy(chunk).start()
+
+    def lower(chunk):
+        pl_wait = pltpu.make_async_remote_copy(
+            src_ref=hidden.at[chunk, 1 - half],
+            dst_ref=hidden.at[chunk, 1 - half],
+            send_sem=hid_send.at[chunk],
+            recv_sem=hid_recv.at[chunk],
+            device_id=(partner, inner),
+            device_id_type=MESH,
+        )
+        pl_wait.wait_recv()
+        units = hidden[chunk].reshape(SLOTS, UPAD)[:, :UNITS]
+        return jnp.dot(units, down_w[...], preferred_element_type=f32).astype(bf16)
+
+    def turn_of(turn):
+        back = (turn * (turn + 1) // 2) % NY
+        return back, (chip_y + NY - back) % NY
+
+    def step(turn, carry):
+        @pl.when(turn < NY)
+        def _():
+            back, chip = turn_of(turn)
+
+            @pl.when(turn > 0)
+            def _():
+                for block in range(NX):
+                    y_copy(back, block).wait_recv()
+                sib_copy(turn, chip).start()
+
+            project(chip * 2 + core)
+            sib_copy(turn, chip).wait_recv()
+            project(chip * 2 + 1 - core)
+
+        @pl.when((turn >= 1) & (turn < NY + 1))
+        def _():
+            back, chip = turn_of(turn - 1)
+            activate(chip * 2 + core)
+            activate(chip * 2 + 1 - core)
+
+        @pl.when(turn >= 2)
+        def _():
+            now = turn - 2
+            back, chip = turn_of(now)
+            sib_out[now] = lower(chip * 2 + 1 - core)
+            fold_copy(now).start()
+            kept = lower(chip * 2 + core).astype(f32)
+            fold_copy(now).wait_recv()
+            kept = kept + sib_in[now].astype(f32)
+
+            @pl.when(now == 0)
+            def _():
+                sum_own[...] = kept
+
+            @pl.when(now > 0)
+            def _():
+                pair_out[now] = kept.astype(bf16)
+                pair_copy(now, back).start()
+
+        return carry
+
+    lax.fori_loop(0, NY + 2, step, 0)
+
+    total = sum_own[...]
+    for turn in range(1, NY):
+        pair_copy(turn, (turn * (turn + 1) // 2) % NY).wait_recv()
+        total = total + pair_in[turn].astype(f32)
+    back_out[...] = total.astype(bf16).reshape(NX, 2 * NZ, HALF)
+
+    def back_copy(ahead):
+        other = (x + ahead) % NX
+        return pltpu.make_async_remote_copy(
+            src_ref=back_out.at[other],
+            dst_ref=back_in.at[x],
+            send_sem=back_send.at[ahead],
+            recv_sem=back_recv.at[ahead],
+            device_id=(other * NZ + z, inner),
+            device_id_type=MESH,
+        )
+
+    for ahead in range(1, NX):
+        back_copy(ahead).start()
+    back_in[x] = back_out[x]
+    for ahead in range(1, NX):
+        back_copy(ahead).wait_recv()
+    answers = back_in[...].reshape(SLOTS, HALF)
+    combined = jnp.dot(mix_matrix(1), answers, preferred_element_type=f32) + jnp.dot(
+        mix_matrix(2), answers, preferred_element_type=f32
+    )
+    mixed_out[...] = combined.reshape(NZ, ROWS, HALF).astype(bf16)
+
+    def mix_copy(index):
+        other = (z + index) % NZ
+        return pltpu.make_async_remote_copy(
+            src_ref=mixed_out.at[other],
+            dst_ref=mixed_in.at[z],
+            send_sem=mix_send.at[index],
+            recv_sem=mix_recv.at[index],
+            device_id=(x * NZ + other, inner),
+            device_id_type=MESH,
+        )
+
+    def start_mix(index, carry):
+        mix_copy(index).start()
+        return carry
+
+    def wait_mix(index, carry):
+        mix_copy(index).wait_recv()
+        return carry
+
+    lax.fori_loop(1, NZ, start_mix, 0)
+    mixed_in[z] = mixed_out[z]
+    lax.fori_loop(1, NZ, wait_mix, 0)
+    both = jnp.sum(mixed_in[...].astype(f32).reshape(NZ // 2, 2, ROWS, HALF), axis=0)
+    for part in range(2):
+        norm[:, part * HALF : (part + 1) * HALF] = both[part]
+    out_ref[...] = (res[...].astype(f32) + norm[...] + bias_term).astype(bf16)
+
 
     for buffer, lane, towards, to, last in lanes:
         for step in range(1, last + 1):
@@ -322,6 +756,34 @@
         att_copy(ahead).wait_send()
     for ahead in (1, 2):
         key_copy(ahead).wait_send()
+
+    def wait_z_sends(index, carry):
+        z_copy(index).wait_send()
+        mix_copy(index).wait_send()
+        return carry
+
+    lax.fori_loop(1, NZ, wait_z_sends, 0)
+    for ahead in range(1, NX):
+        x_copy(ahead).wait_send()
+        back_copy(ahead).wait_send()
+    for ahead in range(1, NY):
+        for block in range(NX):
+            y_copy(ahead, block).wait_send()
+        pair_copy(ahead, (ahead * (ahead + 1) // 2) % NY).wait_send()
+
+    def wait_turn(turn, carry):
+        back, chip = turn_of(turn)
+        sib_copy(turn, chip).wait_send()
+        fold_copy(turn).wait_send()
+        return carry
+
+    def wait_chunk(chunk, carry):
+        gate_copy(chunk).wait_send()
+        hid_copy(chunk).wait_send()
+        return carry
+
+    lax.fori_loop(0, NY, wait_turn, 0)
+    lax.fori_loop(0, NI, wait_chunk, 0)
 
 
 def rope_tables(dp_index):
@@ -337,122 +799,6 @@
     return (
         jnp.concatenate([head_cos, head_cos, head_cos, ones], axis=1),
         jnp.concatenate([head_sin, head_sin, head_sin, 0.0 * ones], axis=1),
-    )
-
-
-def attention_layer(tokens, segments, attn_gain, w_query, w_keyval, sink_logits, w_out):
-    dp_index = lax.axis_index("dp")
-    cos_table, sin_table = rope_tables(dp_index)
-    pad_rows = ((0, KPAD - KPART), (0, 0))
-    w_in = jnp.pad(jnp.concatenate([w_query, w_keyval], axis=1), pad_rows)
-    w_back = jnp.pad(w_out.T, pad_rows)
-    vmem = pl.BlockSpec(memory_space=pltpu.VMEM)
-    width = QCOLS + KVCOLS
-    bf16, f32 = jnp.bfloat16, jnp.float32
-    dma = pltpu.SemaphoreType.DMA
-    return pl.pallas_call(
-        attention_kernel,
-        out_shape=jax.ShapeDtypeStruct((ROWS, D), bf16),
-        in_specs=[vmem] * 7 + [pl.BlockSpec(memory_space=pltpu.SMEM)],
-        out_specs=vmem,
-        scratch_shapes=[
-            pltpu.VMEM((ROWS, D), f32),
-            pltpu.VMEM((ROWS, NX * QUART), f32),
-            pltpu.VMEM((NX, ROWS, QUART), bf16),
-            pltpu.VMEM((NX * NI, ROWS, QUART), bf16),
-            pltpu.VMEM((NZ, KPAD, width), bf16),
-            pltpu.VMEM((NZ, KPAD, QCOLS), bf16),
-            pltpu.VMEM((NX, GROUP, width), f32),
-            pltpu.VMEM((NX, GROUP, width), bf16),
-            pltpu.VMEM((NX - 1, GROUP, width), bf16),
-            pltpu.VMEM((NX, GROUP, 128), f32),
-            pltpu.VMEM((3, GROUP, KVCOLS + 128), bf16),
-            pltpu.VMEM((NX, GROUP, QCOLS), bf16),
-            pltpu.VMEM((NX * NI, ROWS, QUART), bf16),
-            pltpu.VMEM((NX * NI, ROWS, QUART), bf16),
-            dma((4, 8)),
-            dma((4, 8)),
-            dma((NX * NI,)),
-            dma((NX * NI,)),
-            dma((NX - 1,)),
-            dma((NX - 1,)),
-            dma((2,)),
-            dma((2,)),
-            dma((NX - 1,)),
-            dma((NX - 1,)),
-            dma((NX * NI,)),
-            dma((NX * NI,)),
-        ],
-        compiler_params=pltpu.CompilerParams(
-            collective_id=0, has_side_effects=True, vmem_limit_bytes=48 * 2**20
-        ),
-        name="attention",
-    )(
-        tokens,
-        attn_gain.reshape(1, D),
-        segments.astype(f32).reshape(ROWS, 1),
-        w_in,
-        w_back,
-        cos_table,
-        sin_table,
-        sink_logits,
-    )
-
-
-def from_partner(value, axis, apart):
-    mask = 2**apart
-    pairs = [(source, source ^ mask) for source in range(lax.axis_size(axis))]
-    return lax.ppermute(value, axis, pairs)
-
-
-def rms_scale(row_block, gain_vector):
-    values = row_block.astype(jnp.float32)
-    mean_square = jnp.mean(values * values, axis=-1, keepdims=True)
-    return (values * lax.rsqrt(mean_square + EPSILON) * gain_vector).astype(jnp.bfloat16)
-
-
-def slot_numbers(route_block, expert_count):
-    flat_routes = route_block.reshape(-1)
-    onehot = (flat_routes[:, None] == jnp.arange(expert_count, dtype=jnp.int32)[None, :]).astype(
-        jnp.int32
-    )
-    earlier = jnp.cumsum(onehot, axis=0) - onehot
-    return jnp.sum(earlier * onehot, axis=1).reshape(route_block.shape)
-
-
-def route_mix(moe_rows, w_router, route_block):
-    expert_count = w_router.shape[1]
-    logits = jnp.dot(moe_rows, w_router, preferred_element_type=jnp.float32)
-    matches = route_block[:, :, None] == jnp.arange(expert_count, dtype=jnp.int32)[None, None, :]
-    chosen = jnp.sum(jnp.where(matches, logits[:, None, :], 0.0), axis=-1)
-    return (jax.nn.softmax(chosen, axis=-1), matches)
-
-
-def send_table(targets, length):
-    columns = jnp.arange(length, dtype=jnp.int32)
-    return jnp.any(columns[:, None, None] == targets[None, :, :], axis=-1).astype(jnp.bfloat16)
-
-
-def spread_rows(table, row_block, dp_count):
-    placed = jnp.dot(table, row_block, preferred_element_type=jnp.float32)
-    return placed.astype(jnp.bfloat16).reshape(dp_count, -1, row_block.shape[1])
-
-
-def join_rows(returned):
-    dp_count, span, width = returned.shape
-    return returned.reshape(-1, width)
-
-
-def pick_rows(returned, targets, weights):
-    taken = jnp.take(returned, targets, axis=0).astype(jnp.float32)
-    return jnp.sum(weights[:, :, None] * taken, axis=1)
-
-
-def activate(gate_up):
-    gate_part = jnp.minimum(gate_up[:, 0::2], CLAMP_LIMIT)
-    up_part = jnp.clip(gate_up[:, 1::2], -CLAMP_LIMIT, CLAMP_LIMIT)
-    return ((up_part + 1.0) * gate_part * jax.nn.sigmoid(GLU_SLOPE * gate_part)).astype(
-        jnp.bfloat16
     )
 
 
@@ -472,62 +818,102 @@
     w_down,
     b_down,
 ):
-    tok_rows, model_width = tokens.shape
-    dp_count = lax.axis_size("dp")
     dp_index = lax.axis_index("dp")
-    inner_index = lax.axis_index("inner")
-    residual = attention_layer(
-        tokens, segments, attn_gain, w_query, w_keyval, sink_logits, w_out
-    )
-    moe_in = rms_scale(residual, moe_gain)
-    expert_count = w_router.shape[1]
-    capacity = 16 * tok_rows // dp_count
-    half_cap = capacity // 2
-    parity = dp_index % 2
-    expert_id = dp_index // 2
-    half_rows = w_gate_up.shape[0]
-    bias_row = lax.dynamic_slice_in_dim(b_gate_up, expert_id, 1, 0)
-    gate_other, down_other = from_partner((w_gate_up, w_down), "dp", 0)
-    mix, matches = route_mix(moe_in, w_router, routes)
-    expert_mix = jnp.sum(jnp.where(matches, mix[:, :, None], 0.0), axis=1)
-    bias_term = jnp.dot(expert_mix, b_down, precision=lax.Precision.HIGHEST)
-    slot_index = slot_numbers(routes, expert_count)
-    source_flip = (dp_index + inner_index) % 2
-    slot_half = (slot_index // half_cap + source_flip) % 2
-    targets = routes * capacity + slot_half * half_cap + slot_index % half_cap
-    length = expert_count * capacity
-    outgoing = spread_rows(send_table(targets, length), moe_in, dp_count)
-    received = lax.all_to_all(outgoing, "dp", split_axis=0, concat_axis=0, tiled=True)
-    expert_rows = lax.all_gather(received, "inner", axis=0, tiled=True)
-    row_block = expert_rows.reshape(-1, expert_rows.shape[-1])
-    own_cols = lax.dynamic_slice_in_dim(row_block, parity * half_rows, half_rows, 1)
-    other_cols = lax.dynamic_slice_in_dim(row_block, (1 - parity) * half_rows, half_rows, 1)
-    own_part = jnp.dot(own_cols, w_gate_up, preferred_element_type=jnp.float32).astype(jnp.bfloat16)
-    other_part = jnp.dot(other_cols, gate_other, preferred_element_type=jnp.float32).astype(
-        jnp.bfloat16
-    )
-    own_part, other_part = lax.optimization_barrier((own_part, other_part))
-    hidden = activate(own_part.astype(jnp.float32) + other_part.astype(jnp.float32) + bias_row)
-    own_out = jnp.dot(hidden, w_down, preferred_element_type=jnp.float32)
-    other_out = jnp.dot(hidden, down_other, preferred_element_type=jnp.float32)
-    joined = jnp.where(
-        parity == 0,
-        jnp.concatenate([own_out, other_out], axis=1),
-        jnp.concatenate([other_out, own_out], axis=1),
-    )
-    partial_value = joined.astype(jnp.bfloat16)
-    summed = lax.psum_scatter(partial_value, "inner", scatter_dimension=0, tiled=True).astype(
-        jnp.float32
-    )
-    returned = lax.all_to_all(
-        summed.reshape(dp_count, -1, summed.shape[-1]).astype(jnp.bfloat16),
-        "dp",
-        split_axis=0,
-        concat_axis=0,
-        tiled=True,
-    ).astype(jnp.float32)
-    moe_sum = pick_rows(join_rows(returned), targets, mix)
-    return (residual.astype(jnp.float32) + moe_sum + bias_term).astype(jnp.bfloat16)
+    cos_table, sin_table = rope_tables(dp_index)
+    pad_rows = ((0, KPAD - KPART), (0, 0))
+    w_in = jnp.pad(jnp.concatenate([w_query, w_keyval], axis=1), pad_rows)
+    w_back = jnp.pad(w_out.T, pad_rows)
+    vmem = pl.BlockSpec(memory_space=pltpu.VMEM)
+    smem = pl.BlockSpec(memory_space=pltpu.SMEM)
+    anywhere = pl.BlockSpec(memory_space=pl.ANY)
+    width = QCOLS + KVCOLS
+    bf16, f32 = jnp.bfloat16, jnp.float32
+    dma = pltpu.SemaphoreType.DMA
+    buffers = [
+        ((ROWS, D), f32),
+        ((ROWS, NX * QUART), f32),
+        ((NX, ROWS, QUART), bf16),
+        ((NX * NI, ROWS, QUART), bf16),
+        ((NZ, KPAD, width), bf16),
+        ((NZ, KPAD, QCOLS), bf16),
+        ((NX, GROUP, width), f32),
+        ((NX, GROUP, width), bf16),
+        ((NX - 1, GROUP, width), bf16),
+        ((NX, GROUP, 128), f32),
+        ((3, GROUP, KVCOLS + 128), bf16),
+        ((NX, GROUP, QCOLS), bf16),
+        ((NX * NI, ROWS, QUART), bf16),
+        ((NX * NI, ROWS, QUART), bf16),
+    ]
+    semaphores = [(4, 8), (NX * NI,), (NX - 1,), (2,), (NX - 1,), (NX * NI,)]
+    expert_inputs = [
+        ((ROWS, D), bf16),
+        ((D, EXPERTS), bf16),
+        ((HALF, 2 * UNITS), bf16),
+        ((HALF, 2 * UPAD), bf16),
+        ((EXPERTS, 2 * UNITS), f32),
+        ((UNITS, HALF), bf16),
+        ((EXPERTS, D), f32),
+    ]
+    expert_buffers = [
+        ((2, ROWS, HPAD), f32),
+        ((NZ, ROWS, HPAD), bf16),
+        ((NZ, ROWS, HPAD), bf16),
+        ((NX, 2 * NZ, HALF), bf16),
+        ((NI, NX, 2 * NZ, HALF), bf16),
+        ((NI, 2, SLOTS // 2, 2 * UPAD), bf16),
+        ((NI, SLOTS // 2, 2 * UPAD), bf16),
+        ((NI, 2, SLOTS // 2, UPAD), bf16),
+        ((NY, SLOTS, HALF), bf16),
+        ((NY, SLOTS, HALF), bf16),
+        ((NY, SLOTS, HALF), bf16),
+        ((NY, SLOTS, HALF), bf16),
+        ((SLOTS, HALF), f32),
+        ((NX, 2 * NZ, HALF), bf16),
+        ((NX, 2 * NZ, HALF), bf16),
+        ((NZ, ROWS, HALF), bf16),
+        ((NZ, ROWS, HALF), bf16),
+    ]
+    expert_semaphores = [(NZ,), (NX,), (NY, NX), (NY,), (NI,), (NI,), (NY,), (NY,), (NX,), (NZ,)]
+
+    def allocate(shapes):
+        return [pltpu.VMEM(shape, dtype) for shape, dtype in shapes]
+
+    def pairs(shapes):
+        return [dma(shape) for shape in shapes for _ in range(2)]
+
+    return pl.pallas_call(
+        layer_kernel,
+        out_shape=jax.ShapeDtypeStruct((ROWS, D), bf16),
+        in_specs=[vmem] * 7 + [smem] + [vmem] * 2 + [anywhere] * 5,
+        out_specs=vmem,
+        scratch_shapes=allocate(buffers)
+        + pairs(semaphores)
+        + allocate(expert_inputs)
+        + [dma((5,))]
+        + allocate(expert_buffers)
+        + pairs(expert_semaphores),
+        compiler_params=pltpu.CompilerParams(
+            collective_id=0, has_side_effects=True, vmem_limit_bytes=56 * 2**20
+        ),
+        name="layer",
+    )(
+        tokens,
+        attn_gain.reshape(1, D),
+        segments.astype(f32).reshape(ROWS, 1),
+        w_in,
+        w_back,
+        cos_table,
+        sin_table,
+        sink_logits,
+        moe_gain.reshape(1, D),
+        routes,
+        w_router,
+        w_gate_up,
+        b_gate_up,
+        w_down,
+        b_down,
+    )
 
 
 def solution(mesh):

time: 296 us -> 207 us (0.70)
  the two profiles are of different devices: /device:TPU:31 before, /device:TPU:1 now
where the time goes in v2:
time: 207 us; the launch traced here: 206 us
  Pallas kernels  193 us (93%)
  local copies, waits for them, and re-layouts  11 us (5%)
  other arithmetic  2.31 us (1%)
    pallas_call x1, Pallas kernels, per_device(): pl.pallas_call(layer_kernel, out_shape=jax.ShapeDtypeStruct((ROWS, D), bf...  193 us
    unnamed x3, local copies, waits for them, and re-layouts  4.83 us

profile of v2, /device:TPU:1, one launch (start us, length us, event | category | flops | bytes accessed | tf_op | source)
XLA Modules:
  0.0 206.3 jit_solution(11339688013944757366)
XLA Ops:
  0.0 0.7 convert_bitcast_fusion
  0.7 0.7 copy.15.seg_ref
  1.3 1.3 copy.16.routes_ref
  2.7 1.3 reshape.19.gain_ref
  4.0 1.3 reshape.21.moe_gain_ref
  5.3 1.4 pad.9.wout_ref
  6.7 1.4 fusion.2.wqkv_ref
  8.2 0.2 multiply_sine_fusion
  8.4 0.7 concatenate.15.sin_ref
  9.1 0.7 concatenate.14.cos_ref
  9.8 2.1 %copy.17.router_hbm = bf16[2880,32]{1,0:T(8,128)(2,1)} copy(bf16[2880,32]{0,1:T(8,128)(2,1)} %param.22) | data formatting | bytes 368640 | tf_op args[8]
  11.9 193.0 %layer.1 = bf16[8,2880]{1,0:T(8,128)(2,1)} custom-call(bf16[8,2880]{1,0:T(8,128)(2,1)} %tok_ref.1, f32[1,2880]{1,0:T(1,128)} %reshape.19.gain_ref, f32[8,1]{1,0:T(8,128)} %copy.15.seg_ref, bf16[48,640]{1,0:T(8,128)(2,1)} %fusion.2.wqkv_ref, bf16[48,512]{1,0:T(8,128)(2,1)} %pad.9.wout_ref, f32[64,256]{1,0:T(8,128)} %concatenate.14.cos_ref, ...), custom_call_target="tpu_custom_call" | custom-call | tf_op jit(solution)/shard_map/layer/pallas_call | solution.py:885
  204.9 1.4 copy.19
  (4 shorter events, 0.0 us)

commit v3 on v2

--- a/solution.py
+++ b/solution.py
@@ -23,7 +23,9 @@
 GROUP = ROWS * NI
 KPART = 45
 KPAD = 48
-QUART = NZ * KPAD
+TEAM = 2 * NX
+RING = NZ // 2
+QUART = RING * KPAD
 HEADS_HERE = 8
 QCOLS = HEADS_HERE * HEAD_DIM
 KVCOLS = 2 * HEAD_DIM
@@ -39,11 +41,17 @@
 NY = 4
 
 
+def places(block):
+    part = 2 * (block // NZ) + block % 2
+    return part * QUART + (block % NZ) // 2 * KPAD, block * KPART
+
+
 def layer_kernel(
     tok_ref,
     gain_ref,
     seg_ref,
-    wqkv_ref,
+    wq_ref,
+    wkv_ref,
     wout_ref,
     cos_ref,
     sin_ref,
@@ -132,18 +140,24 @@
     inner = lax.axis_index("inner")
     x = dp // NZ
     z = dp % NZ
-    right = x * NZ + (z + 1) % NZ
-    left = x * NZ + (z + NZ - 1) % NZ
+    right = x * NZ + (z + 2) % NZ
+    left = x * NZ + (z + NZ - 2) % NZ
+    spot = z // 2
+    team = 2 * x + z % 2
+
+    def member(ahead):
+        other = (team + ahead) % TEAM
+        return other, (other // 2) * NZ + 2 * spot + other % 2
 
     barrier = pltpu.get_barrier_semaphore()
 
     def greet(index, carry):
-        other_dp = ((x + index // NI) % NX) * NZ + z
+        other, other_dp = member(index // NI)
         other_in = (inner + index % NI) % NI
         pl.semaphore_signal(barrier, inc=1, device_id=(other_dp, other_in), device_id_type=MESH)
         return carry
 
-    lax.fori_loop(1, NX * NI, greet, 0)
+    lax.fori_loop(1, TEAM * NI, greet, 0)
 
     def greet_z(index, carry):
         other = x * NZ + (z + index) % NZ
@@ -173,12 +187,24 @@
     ]
     for load in loads:
         load.start()
-    wq_all[z] = wqkv_ref[...]
-    wo_all[z] = wout_ref[...]
-    pl.semaphore_wait(barrier, NX * NI - 1 + NZ - 1 + 4)
+    widen = jnp.where(
+        lax.broadcasted_iota(jnp.int32, (KPAD, KPART), 0)
+        == lax.broadcasted_iota(jnp.int32, (KPAD, KPART), 1),
+        1.0,
+        0.0,
+    ).astype(jnp.bfloat16)
+    for source, target, low, high in (
+        (wq_ref, wq_all, 0, QCOLS),
+        (wkv_ref, wq_all, QCOLS, QCOLS + KVCOLS),
+        (wout_ref, wo_all, 0, QCOLS),
+    ):
+        target[spot, :, low:high] = jnp.dot(
+            widen, source[...], preferred_element_type=jnp.float32
+        ).astype(jnp.bfloat16)
+    pl.semaphore_wait(barrier, TEAM * NI - 1 + NZ - 1 + 4)
 
     def ring(buffer, lane, step, towards, to):
-        owner = (z + NZ - towards * (step - 1)) % NZ
+        owner = (spot + RING - towards * (step - 1)) % RING
         return pltpu.make_async_remote_copy(
             src_ref=buffer.at[owner],
             dst_ref=buffer.at[owner],
@@ -189,34 +215,41 @@
         )
 
     lanes = (
-        (wq_all, 0, 1, right, 8),
-        (wq_all, 1, -1, left, 7),
-        (wo_all, 2, 1, right, 7),
-        (wo_all, 3, -1, left, 8),
+        (wq_all, 0, 1, right, 4),
+        (wq_all, 1, -1, left, 3),
+        (wo_all, 2, 1, right, 3),
+        (wo_all, 3, -1, left, 4),
     )
     for buffer, lane, towards, to, last in lanes:
         ring(buffer, lane, 1, towards, to).start()
 
     values = tok_ref[...].astype(jnp.float32)
     mean_square = jnp.mean(values * values, axis=-1, keepdims=True)
-    norm[...] = values * lax.rsqrt(mean_square + EPSILON) * gain_ref[...]
+    norm[...] = values * lax.rsqrt(mean_square + EPSILON) * gain_ref[...].reshape(1, D)
     wide[...] = jnp.zeros_like(wide)
     for block in range(NX * NZ):
-        wide[:, block * KPAD : block * KPAD + KPART] = norm[:, block * KPART : (block + 1) * KPART]
-    for part in range(NX):
-        wide[:, part * QUART + KPART : part * QUART + KPART + 1] = seg_ref[...]
-    for part in range(NX):
+        wide_at, block_at = places(block)
+        wide[:, wide_at : wide_at + KPART] = norm[:, block_at : block_at + KPART]
+    row_number = lax.broadcasted_iota(jnp.int32, (ROWS, 1), 0)
+    own_segments = jnp.zeros((ROWS, 1), jnp.float32)
+    for number in range(ROWS):
+        own_segments = jnp.where(
+            row_number == number, seg_ref[number].astype(jnp.float32), own_segments
+        )
+    for part in range(TEAM):
+        wide[:, part * QUART + KPART : part * QUART + KPART + 1] = own_segments
+    for part in range(TEAM):
         quarter[part] = wide[:, part * QUART : (part + 1) * QUART].astype(jnp.bfloat16)
 
     def row_copy(index):
-        other_x = (x + index // NI) % NX
+        other, other_dp = member(index // NI)
         other_in = (inner + index % NI) % NI
         return pltpu.make_async_remote_copy(
-            src_ref=quarter.at[other_x],
-            dst_ref=rows_in.at[x * NI + inner],
+            src_ref=quarter.at[other],
+            dst_ref=rows_in.at[team * NI + inner],
             send_sem=row_send.at[index],
             recv_sem=row_recv.at[index],
-            device_id=(other_x * NZ + z, other_in),
+            device_id=(other_dp, other_in),
             device_id_type=MESH,
         )
 
@@ -224,10 +257,10 @@
         row_copy(index).start()
         return carry
 
-    lax.fori_loop(1, NX * NI, start_row, 0)
-    rows_in[x * NI + inner] = quarter[x]
-
-    for step in range(1, 9):
+    lax.fori_loop(1, TEAM * NI, start_row, 0)
+    rows_in[team * NI + inner] = quarter[team]
+
+    for step in range(1, RING // 2 + 1):
         for buffer, lane, towards, to, last in lanes:
             if step <= last:
                 ring(buffer, lane, step, towards, to).wait_recv()
@@ -238,33 +271,33 @@
         row_copy(index).wait_recv()
         return carry
 
-    lax.fori_loop(1, NX * NI, wait_row, 0)
-
-    all_rows = rows_in[...].astype(jnp.float32).reshape(NX * GROUP, QUART)
-    seg_f[...] = all_rows[:, :128].reshape(NX, GROUP, 128)
+    lax.fori_loop(1, TEAM * NI, wait_row, 0)
+
+    all_rows = rows_in[...].astype(jnp.float32).reshape(TEAM * GROUP, QUART)
+    seg_f[...] = all_rows[:, :128].reshape(TEAM, GROUP, 128)
     product = jnp.dot(
         all_rows.astype(jnp.bfloat16),
         wq_all[...].reshape(QUART, QCOLS + KVCOLS),
         preferred_element_type=jnp.float32,
-    ).reshape(NX, GROUP, QCOLS + KVCOLS)
+    ).reshape(TEAM, GROUP, QCOLS + KVCOLS)
     part_f[...] = product
     part_out[...] = product.astype(jnp.bfloat16)
 
     def part_copy(ahead):
-        other = (x + ahead) % NX
+        other, other_dp = member(ahead)
         return pltpu.make_async_remote_copy(
             src_ref=part_out.at[other],
             dst_ref=part_in.at[ahead - 1],
             send_sem=part_send.at[ahead - 1],
             recv_sem=part_recv.at[ahead - 1],
-            device_id=(other * NZ + z, inner),
-            device_id_type=MESH,
-        )
-
-    for ahead in range(1, NX):
+            device_id=(other_dp, inner),
+            device_id_type=MESH,
+        )
+
+    for ahead in range(1, TEAM):
         part_copy(ahead).start()
-    total = part_f[x]
-    for ahead in range(1, NX):
+    total = part_f[team]
+    for ahead in range(1, TEAM):
         part_copy(ahead).wait_recv()
         total = total + part_in[ahead - 1].astype(jnp.float32)
 
@@ -278,7 +311,7 @@
         pltpu.roll(total, HEAD_DIM // 2, 1),
     )
     turned = (total * cosine + swapped * sine).astype(jnp.bfloat16)
-    own_seg = seg_f[x][:, KPART : KPART + 1]
+    own_seg = seg_f[team][:, KPART : KPART + 1]
     keyval[2, :, :KVCOLS] = turned[:, QCOLS:]
     keyval[2, :, KVCOLS:] = jnp.broadcast_to(own_seg, (GROUP, 128)).astype(jnp.bfloat16)
 
@@ -331,39 +364,39 @@
         denominator = jnp.sum(weights, axis=-1, keepdims=True) + jnp.exp(sink - row_max)
         probabilities = (weights / denominator).astype(jnp.bfloat16)
         mixed = jnp.dot(probabilities, value_block, preferred_element_type=jnp.float32)
-        attended[x, :, head * HEAD_DIM : (head + 1) * HEAD_DIM] = mixed.astype(jnp.bfloat16)
+        attended[team, :, head * HEAD_DIM : (head + 1) * HEAD_DIM] = mixed.astype(jnp.bfloat16)
 
     def att_copy(ahead):
         return pltpu.make_async_remote_copy(
-            src_ref=attended.at[x],
-            dst_ref=attended.at[x],
+            src_ref=attended.at[team],
+            dst_ref=attended.at[team],
             send_sem=att_send.at[ahead - 1],
             recv_sem=att_recv.at[ahead - 1],
-            device_id=(((x + ahead) % NX) * NZ + z, inner),
-            device_id_type=MESH,
-        )
-
-    for ahead in range(1, NX):
+            device_id=(member(ahead)[1], inner),
+            device_id_type=MESH,
+        )
+
+    for ahead in range(1, TEAM):
         att_copy(ahead).start()
-    for ahead in range(1, NX):
+    for ahead in range(1, TEAM):
         att_copy(ahead).wait_recv()
     projected = lax.dot_general(
-        attended[...].reshape(NX * GROUP, QCOLS),
+        attended[...].reshape(TEAM * GROUP, QCOLS),
         wo_all[...].reshape(QUART, QCOLS),
         nt,
         preferred_element_type=jnp.float32,
     )
-    out_part[...] = projected.reshape(NX * NI, ROWS, QUART).astype(jnp.bfloat16)
+    out_part[...] = projected.reshape(TEAM * NI, ROWS, QUART).astype(jnp.bfloat16)
 
     def out_copy(index):
-        other_x = (x + index // NI) % NX
+        other, other_dp = member(index // NI)
         other_in = (inner + index % NI) % NI
         return pltpu.make_async_remote_copy(
-            src_ref=out_part.at[other_x * NI + other_in],
-            dst_ref=out_in.at[x * NI + inner],
+            src_ref=out_part.at[other * NI + other_in],
+            dst_ref=out_in.at[team * NI + inner],
             send_sem=out_send.at[index],
             recv_sem=out_recv.at[index],
-            device_id=(other_x * NZ + z, other_in),
+            device_id=(other_dp, other_in),
             device_id_type=MESH,
         )
 
@@ -375,16 +408,17 @@
         out_copy(index).wait_recv()
         return carry
 
-    lax.fori_loop(1, NX * NI, start_out, 0)
-    out_in[x * NI + inner] = out_part[x * NI + inner]
-    lax.fori_loop(1, NX * NI, wait_out, 0)
+    lax.fori_loop(1, TEAM * NI, start_out, 0)
+    out_in[team * NI + inner] = out_part[team * NI + inner]
+    lax.fori_loop(1, TEAM * NI, wait_out, 0)
     summed = jnp.sum(
-        out_in[...].astype(jnp.float32).reshape(NX, NI, ROWS, QUART), axis=1
-    )
-    for part in range(NX):
+        out_in[...].astype(jnp.float32).reshape(TEAM, NI, ROWS, QUART), axis=1
+    )
+    for part in range(TEAM):
         wide[:, part * QUART : (part + 1) * QUART] = summed[part]
     for block in range(NX * NZ):
-        norm[:, block * KPART : (block + 1) * KPART] = wide[:, block * KPAD : block * KPAD + KPART]
+        wide_at, block_at = places(block)
+        norm[:, block_at : block_at + KPART] = wide[:, wide_at : wide_at + KPART]
     res[...] = (tok_ref[...].astype(jnp.float32) + norm[...]).astype(jnp.bfloat16)
 
     bf16, f32 = jnp.bfloat16, jnp.float32
@@ -406,15 +440,23 @@
 
     values = res[...].astype(f32)
     mean_square = jnp.mean(values * values, axis=-1, keepdims=True)
-    moe_in = (values * lax.rsqrt(mean_square + EPSILON) * moe_gain_ref[...]).astype(bf16)
+    moe_in = (values * lax.rsqrt(mean_square + EPSILON) * moe_gain_ref[...].reshape(1, D)).astype(bf16)
     norm[...] = moe_in.astype(f32)
     halves[...] = jnp.zeros_like(halves)
     for part in range(2):
         halves[part, :, :HALF] = norm[:, part * HALF : (part + 1) * HALF]
 
-    logits = jnp.dot(moe_in, router[...], preferred_element_type=f32)
+    logits = lax.dot_general(moe_in, router[...], nt, preferred_element_type=f32)
     expert = iota((ROWS, EXPERTS), 1)
-    named = [ones_where(routes_ref[:, k : k + 1] == expert) for k in range(4)]
+    route_row = iota((ROWS, EXPERTS), 0)
+    named = []
+    for k in range(4):
+        match = jnp.zeros((ROWS, EXPERTS), f32)
+        for number in range(ROWS):
+            match = jnp.where(
+                (route_row == number) & (expert == routes_ref[k, number]), 1.0, match
+            )
+        named.append(match)
     chosen = [jnp.sum(match * logits, axis=-1, keepdims=True) for match in named]
     largest = jnp.maximum(jnp.maximum(chosen[0], chosen[1]), jnp.maximum(chosen[2], chosen[3]))
     raised = [jnp.exp(value - largest) for value in chosen]
@@ -546,6 +588,18 @@
             device_id_type=MESH,
         )
 
+    def pass_copy(ahead, back):
+        chip = (chip_y + NY - ahead) % NY
+        block = rows_all.at[chip * 2 + core, (x + NX - back) % NX]
+        return pltpu.make_async_remote_copy(
+            src_ref=block,
+            dst_ref=block,
+            send_sem=y_send.at[2, back],
+            recv_sem=y_recv.at[2, back],
+            device_id=(dp, ((chip_y + ahead) % NY) * 2 + core),
+            device_id_type=MESH,
+        )
+
     def sib_copy(turn, chip):
         chunk = rows_all.at[chip * 2 + core]
         return pltpu.make_async_remote_copy(
@@ -563,7 +617,7 @@
     for back in range(NX):
         if back:
             x_copy(back).wait_recv()
-        for ahead in (1, 3, 2):
+        for ahead in (1, 3):
             y_copy(ahead, back).start()
     sib_copy(0, chip_y).start()
 
@@ -650,6 +704,11 @@
             def _():
                 for block in range(NX):
                     y_copy(back, block).wait_recv()
+
+                    @pl.when(back == (1 if block < 2 else 3))
+                    def _():
+                        pass_copy(back, block).start()
+
                 sib_copy(turn, chip).start()
 
             project(chip * 2 + core)
@@ -750,8 +809,8 @@
         out_copy(index).wait_send()
         return carry
 
-    lax.fori_loop(1, NX * NI, wait_sends, 0)
-    for ahead in range(1, NX):
+    lax.fori_loop(1, TEAM * NI, wait_sends, 0)
+    for ahead in range(1, TEAM):
         part_copy(ahead).wait_send()
         att_copy(ahead).wait_send()
     for ahead in (1, 2):
@@ -768,7 +827,10 @@
         back_copy(ahead).wait_send()
     for ahead in range(1, NY):
         for block in range(NX):
-            y_copy(ahead, block).wait_send()
+            if ahead != 2:
+                y_copy(ahead, block).wait_send()
+            else:
+                pass_copy(1 if block < 2 else 3, block).wait_send()
         pair_copy(ahead, (ahead * (ahead + 1) // 2) % NY).wait_send()
 
     def wait_turn(turn, carry):
@@ -820,9 +882,6 @@
 ):
     dp_index = lax.axis_index("dp")
     cos_table, sin_table = rope_tables(dp_index)
-    pad_rows = ((0, KPAD - KPART), (0, 0))
-    w_in = jnp.pad(jnp.concatenate([w_query, w_keyval], axis=1), pad_rows)
-    w_back = jnp.pad(w_out.T, pad_rows)
     vmem = pl.BlockSpec(memory_space=pltpu.VMEM)
     smem = pl.BlockSpec(memory_space=pltpu.SMEM)
     anywhere = pl.BlockSpec(memory_space=pl.ANY)
@@ -831,24 +890,24 @@
     dma = pltpu.SemaphoreType.DMA
     buffers = [
         ((ROWS, D), f32),
-        ((ROWS, NX * QUART), f32),
-        ((NX, ROWS, QUART), bf16),
-        ((NX * NI, ROWS, QUART), bf16),
-        ((NZ, KPAD, width), bf16),
-        ((NZ, KPAD, QCOLS), bf16),
-        ((NX, GROUP, width), f32),
-        ((NX, GROUP, width), bf16),
-        ((NX - 1, GROUP, width), bf16),
-        ((NX, GROUP, 128), f32),
+        ((ROWS, TEAM * QUART), f32),
+        ((TEAM, ROWS, QUART), bf16),
+        ((TEAM * NI, ROWS, QUART), bf16),
+        ((RING, KPAD, width), bf16),
+        ((RING, KPAD, QCOLS), bf16),
+        ((TEAM, GROUP, width), f32),
+        ((TEAM, GROUP, width), bf16),
+        ((TEAM - 1, GROUP, width), bf16),
+        ((TEAM, GROUP, 128), f32),
         ((3, GROUP, KVCOLS + 128), bf16),
-        ((NX, GROUP, QCOLS), bf16),
-        ((NX * NI, ROWS, QUART), bf16),
-        ((NX * NI, ROWS, QUART), bf16),
+        ((TEAM, GROUP, QCOLS), bf16),
+        ((TEAM * NI, ROWS, QUART), bf16),
+        ((TEAM * NI, ROWS, QUART), bf16),
     ]
-    semaphores = [(4, 8), (NX * NI,), (NX - 1,), (2,), (NX - 1,), (NX * NI,)]
+    semaphores = [(4, 4), (TEAM * NI,), (TEAM - 1,), (2,), (TEAM - 1,), (TEAM * NI,)]
     expert_inputs = [
         ((ROWS, D), bf16),
-        ((D, EXPERTS), bf16),
+        ((EXPERTS, D), bf16),
         ((HALF, 2 * UNITS), bf16),
         ((HALF, 2 * UPAD), bf16),
         ((EXPERTS, 2 * UNITS), f32),
@@ -885,7 +944,7 @@
     return pl.pallas_call(
         layer_kernel,
         out_shape=jax.ShapeDtypeStruct((ROWS, D), bf16),
-        in_specs=[vmem] * 7 + [smem] + [vmem] * 2 + [anywhere] * 5,
+        in_specs=[vmem] * 2 + [smem] + [vmem] * 5 + [smem, vmem, smem] + [anywhere] * 5,
         out_specs=vmem,
         scratch_shapes=allocate(buffers)
         + pairs(semaphores)
@@ -899,16 +958,17 @@
         name="layer",
     )(
         tokens,
-        attn_gain.reshape(1, D),
-        segments.astype(f32).reshape(ROWS, 1),
-        w_in,
-        w_back,
+        attn_gain,
+        segments,
+        w_query,
+        w_keyval,
+        w_out.T,
         cos_table,
         sin_table,
         sink_logits,
-        moe_gain.reshape(1, D),
-        routes,
-        w_router,
+        moe_gain,
+        routes.T,
+        w_router.T,
         w_gate_up,
         b_gate_up,
         w_down,

time: 207 us -> 191 us (0.923)
  local copies, waits for them, and re-layouts: 11 us -> 2.88 us
  Pallas kernels: 193 us -> 186 us
  other arithmetic: 2.31 us -> 0.21 us
    pallas_call x1, Pallas kernels: 193 us -> 186 us  [per_device(): pl.pallas_call(layer_kernel, out_shape=jax.ShapeDtypeStruct((ROWS, D), bf...]
    unnamed x3 -> x1, local copies, waits for them, and re-layouts: 4.83 us -> 1.42 us
    reshape x3 -> x0, local copies, waits for them, and re-layouts: 3.3 us -> none  [the longest x1 1.31 us: per_device(): attn_gain.reshape(1, D)]
where the time goes in v3:
time: 191 us; the launch traced here: 189 us
  Pallas kernels  186 us (97%)
  local copies, waits for them, and re-layouts  2.88 us (2%)
    pallas_call x1, Pallas kernels, per_device(): pl.pallas_call(layer_kernel, out_shape=jax.ShapeDtypeStruct((ROWS, D), bf...  186 us

profile of v3, /device:TPU:1, one launch (start us, length us, event | category | flops | bytes accessed | tf_op | source)
XLA Modules:
  0.0 189.1 jit_solution(12439463652478351377)
XLA Ops:
  0.0 0.2 multiply_sine_fusion
  0.2 0.7 concatenate.11.sin_ref
  1.0 0.7 concatenate.10.cos_ref
  1.7 186.0 %layer.1 = bf16[8,2880]{1,0:T(8,128)(2,1)} custom-call(bf16[8,2880]{1,0:T(8,128)(2,1)} %tok_ref.1, f32[2880]{0:T(1024)} %gain_ref.1, s32[8]{0:T(128)} %seg_ref.1, bf16[45,512]{1,0:T(8,128)(2,1)} %wq_ref.1, bf16[45,128]{1,0:T(8,128)(2,1)} %wkv_ref.1, bf16[45,512]{1,0:T(8,128)(2,1)} %bitcast.4, f32[64,256]{1,0:T(8,128)} %concatenate.10.cos_ref, ...), custom_call_target="tpu_custom_call" | custom-call | tf_op jit(solution)/shard_map/layer/pallas_call | solution.py:944
  187.7 1.4 copy.16
  (4 shorter events, 0.0 us)

commit v4 on v3

--- a/solution.py
+++ b/solution.py
@@ -712,24 +712,33 @@
                 sib_copy(turn, chip).start()
 
             project(chip * 2 + core)
-            sib_copy(turn, chip).wait_recv()
-            project(chip * 2 + 1 - core)
 
         @pl.when((turn >= 1) & (turn < NY + 1))
         def _():
             back, chip = turn_of(turn - 1)
+            sib_copy(turn - 1, chip).wait_recv()
+            project(chip * 2 + 1 - core)
+
+        @pl.when((turn >= 2) & (turn < NY + 2))
+        def _():
+            back, chip = turn_of(turn - 2)
             activate(chip * 2 + core)
             activate(chip * 2 + 1 - core)
 
-        @pl.when(turn >= 2)
+        @pl.when((turn >= 3) & (turn < NY + 3))
         def _():
-            now = turn - 2
+            now = turn - 3
             back, chip = turn_of(now)
             sib_out[now] = lower(chip * 2 + 1 - core)
             fold_copy(now).start()
-            kept = lower(chip * 2 + core).astype(f32)
+            pair_out[now] = lower(chip * 2 + core)
+
+        @pl.when(turn >= 4)
+        def _():
+            now = turn - 4
+            back, chip = turn_of(now)
             fold_copy(now).wait_recv()
-            kept = kept + sib_in[now].astype(f32)
+            kept = pair_out[now].astype(f32) + sib_in[now].astype(f32)
 
             @pl.when(now == 0)
             def _():
@@ -742,7 +751,9 @@
 
         return carry
 
-    lax.fori_loop(0, NY + 2, step, 0)
+    mix_high_rows = mix_matrix(1)
+    mix_low_rows = mix_matrix(2)
+    lax.fori_loop(0, NY + 4, step, 0)
 
     total = sum_own[...]
     for turn in range(1, NY):
@@ -767,8 +778,8 @@
     for ahead in range(1, NX):
         back_copy(ahead).wait_recv()
     answers = back_in[...].reshape(SLOTS, HALF)
-    combined = jnp.dot(mix_matrix(1), answers, preferred_element_type=f32) + jnp.dot(
-        mix_matrix(2), answers, preferred_element_type=f32
+    combined = jnp.dot(mix_high_rows, answers, preferred_element_type=f32) + jnp.dot(
+        mix_low_rows, answers, preferred_element_type=f32
     )
     mixed_out[...] = combined.reshape(NZ, ROWS, HALF).astype(bf16)
 

time: 191 us -> 191 us (level)
  no operation moved by 1% of the time
where the time goes in v4:
time: 191 us; the launch traced here: 189 us
  Pallas kernels  186 us (97%)
  local copies, waits for them, and re-layouts  2.88 us (2%)
    pallas_call x1, Pallas kernels, per_device(): pl.pallas_call(layer_kernel, out_shape=jax.ShapeDtypeStruct((ROWS, D), bf...  186 us

profile of v4, /device:TPU:1, one launch (start us, length us, event | category | flops | bytes accessed | tf_op | source)
XLA Modules:
  0.0 189.3 jit_solution(2371499537970283171)
XLA Ops:
  0.0 0.2 multiply_sine_fusion
  0.2 0.7 concatenate.11.sin_ref
  1.0 0.7 concatenate.10.cos_ref
  1.7 186.2 %layer.1 = bf16[8,2880]{1,0:T(8,128)(2,1)} custom-call(bf16[8,2880]{1,0:T(8,128)(2,1)} %tok_ref.1, f32[2880]{0:T(1024)} %gain_ref.1, s32[8]{0:T(128)} %seg_ref.1, bf16[45,512]{1,0:T(8,128)(2,1)} %wq_ref.1, bf16[45,128]{1,0:T(8,128)(2,1)} %wkv_ref.1, bf16[45,512]{1,0:T(8,128)(2,1)} %bitcast.4, f32[64,256]{1,0:T(8,128)} %concatenate.10.cos_ref, ...), custom_call_target="tpu_custom_call" | custom-call | tf_op jit(solution)/shard_map/layer/pallas_call | solution.py:955
  187.9 1.4 copy.16
  (4 shorter events, 0.0 us)

commit v5 on v4

--- a/solution.py
+++ b/solution.py
@@ -503,8 +503,11 @@
             device_id_type=MESH,
         )
 
+    def far_first(index):
+        return NZ // 2 + (index // 2) * (2 * (index % 2) - 1)
+
     def start_z(index, carry):
-        z_copy(index).start()
+        z_copy(far_first(index)).start()
         return carry
 
     def wait_z(index, carry):
@@ -795,7 +798,7 @@
         )
 
     def start_mix(index, carry):
-        mix_copy(index).start()
+        mix_copy(far_first(index)).start()
         return carry
 
     def wait_mix(index, carry):

time: 191 us -> 189 us (0.990)
  Pallas kernels: 186 us -> 184 us
    pallas_call x1, Pallas kernels: 186 us -> 184 us  [per_device(): pl.pallas_call(layer_kernel, out_shape=jax.ShapeDtypeStruct((ROWS, D), bf...]
where the time goes in v5:
time: 189 us; the launch traced here: 187 us
  Pallas kernels  184 us (97%)
  local copies, waits for them, and re-layouts  2.88 us (2%)
    pallas_call x1, Pallas kernels, per_device(): pl.pallas_call(layer_kernel, out_shape=jax.ShapeDtypeStruct((ROWS, D), bf...  184 us

profile of v5, /device:TPU:1, one launch (start us, length us, event | category | flops | bytes accessed | tf_op | source)
XLA Modules:
  0.0 187.3 jit_solution(638837775818109134)
XLA Ops:
  0.0 0.2 multiply_sine_fusion
  0.2 0.7 concatenate.11.sin_ref
  1.0 0.7 concatenate.10.cos_ref
  1.7 184.2 %layer.1 = bf16[8,2880]{1,0:T(8,128)(2,1)} custom-call(bf16[8,2880]{1,0:T(8,128)(2,1)} %tok_ref.1, f32[2880]{0:T(1024)} %gain_ref.1, s32[8]{0:T(128)} %seg_ref.1, bf16[45,512]{1,0:T(8,128)(2,1)} %wq_ref.1, bf16[45,128]{1,0:T(8,128)(2,1)} %wkv_ref.1, bf16[45,512]{1,0:T(8,128)(2,1)} %bitcast.4, f32[64,256]{1,0:T(8,128)} %concatenate.10.cos_ref, ...), custom_call_target="tpu_custom_call" | custom-call | tf_op jit(solution)/shard_map/layer/pallas_call | solution.py:958
  185.9 1.4 copy.16
  (4 shorter events, 0.0 us)
